TPU v7x, 32 devices: a whole 2x2x4 slice. The times are simulated.
32 devices in a mesh: wide: 8 (over z, x), narrow: 4 (over y, core).
Axes of the slice: x: 2, y: 2, z: 4, core: 2. Of those that a mesh axis runs over, the one named last changes fastest.
Arguments:
- fields: bfloat16 [256, 32768], P('wide', 'narrow'), may hold values from -8 to 8
- counts: int32 [4, 8], P(None, 'wide'), may hold values from 1 to 8, as said below
- obs_index: int32 [4, 8, 8, 512], P('narrow', 'wide'), may hold values from 0 to 1023
- obs_value: float32 [4, 8, 8, 512], P('narrow', 'wide'), may hold values from -6 to 6
- obs_weight: bfloat16 [4, 8, 8, 512], P('narrow', 'wide'), may hold values from 1 to 16
Outputs:
- analysis: bfloat16 [256, 32768], P('wide', 'narrow')
Inputs may be any that keep to these rules, and one draw needn't show every extreme that they name: `counts`: tiles with the same wide index form a group of 4; in each group exactly one tile owns 6 to 8 patches and every other tile owns 1 to 4. `obs_index`: slots numbered at or beyond the tile's count are never read.
All inputs are finite; a program needn't handle non-finite values.
Results may differ from a plain program's by a relative error of at most 0.009.
Values may be sent and summed in bfloat16 or wider, within the bound.
No kernel may reach another device: no remote copies, remote signals or barrier semaphores. Data moves between devices by JAX's collectives and lax.ppermute only.
A program may use at most 64 MiB of HBM per device.

v0:
```python
import jax
import jax.numpy as jnp
from jax import lax
from jax.sharding import PartitionSpec as P

NS_ITERS = 6


def prepare_slots(observed, weighted, innovation):
    members = observed.shape[0]
    identity_matrix = jnp.eye(members, dtype=jnp.float32)
    gram_matrix = jnp.einsum("ksn,lsn->skl", weighted, observed, preferred_element_type=jnp.float32)
    gram_matrix = gram_matrix + (members - 1.0) * identity_matrix
    scale_value = jnp.sqrt(jnp.sum(gram_matrix * gram_matrix, axis=(1, 2)))
    right_side = jnp.einsum("ksn,sn->sk", observed, innovation, preferred_element_type=jnp.float32)
    iterate = (gram_matrix / scale_value[:, None, None]).astype(jnp.bfloat16)
    return (iterate, scale_value, right_side)


def newton_steps(iterate):
    members = iterate.shape[1]
    identity_matrix = jnp.eye(members, dtype=jnp.float32)
    root_matrix = jnp.broadcast_to(identity_matrix.astype(jnp.bfloat16), iterate.shape)
    for iteration in range(NS_ITERS):
        product = jnp.einsum(
            "skl,slm->skm", root_matrix, iterate, preferred_element_type=jnp.float32
        )
        factor = (1.5 * identity_matrix - 0.5 * product).astype(jnp.bfloat16)
        next_iterate = jnp.einsum(
            "skl,slm->skm", iterate, factor, preferred_element_type=jnp.float32
        ).astype(jnp.bfloat16)
        root_matrix = jnp.einsum(
            "skl,slm->skm", factor, root_matrix, preferred_element_type=jnp.float32
        ).astype(jnp.bfloat16)
        iterate = next_iterate
    return root_matrix


def finish_slots(root_matrix, scale_value, right_side):
    members = root_matrix.shape[1]
    root_float = root_matrix.astype(jnp.float32)
    inner_vector = jnp.einsum("skl,sl->sk", root_float, right_side, precision=lax.Precision.HIGHEST)
    mean_shift = (
        jnp.einsum("skl,sl->sk", root_float, inner_vector, precision=lax.Precision.HIGHEST)
        / scale_value[:, None]
    )
    patch_weight = (
        jnp.sqrt((members - 1.0) / scale_value)[:, None, None] * root_float + mean_shift[:, :, None]
    )
    return patch_weight.astype(jnp.bfloat16)


def solve_slots(observed, weighted, innovation):
    iterate, scale_value, right_side = prepare_slots(observed, weighted, innovation)
    return finish_slots(newton_steps(iterate), scale_value, right_side)


def combine_blocks(anomaly, member_mean, patch_weights, patch_count):
    members, cell_total = anomaly.shape
    slot_total = patch_weights.shape[0]
    block_ids = jnp.arange(slot_total, dtype=jnp.int32)
    owner_patch = block_ids * patch_count // slot_total
    pick_table = (owner_patch[:, None] == block_ids[None, :]).astype(jnp.bfloat16)
    chosen = jnp.einsum(
        "bp,pkl->bkl", pick_table, patch_weights, preferred_element_type=jnp.float32
    ).astype(jnp.bfloat16)
    blocks = anomaly.reshape(members, slot_total, cell_total // slot_total)
    result = jnp.einsum("bkl,kbc->lbc", chosen, blocks, preferred_element_type=jnp.float32)
    result = result + member_mean.reshape(1, slot_total, cell_total // slot_total)
    return result.reshape(members, cell_total).astype(jnp.bfloat16)


def per_device(fields, counts, obs_index, obs_value, obs_weight):
    tile_fields = lax.all_to_all(fields, "wide", split_axis=1, concat_axis=0, tiled=True)
    members = tile_fields.shape[0]
    member_mean = jnp.sum(tile_fields, axis=0, dtype=jnp.float32) / members
    anomaly = (tile_fields - member_mean[None, :]).astype(jnp.bfloat16)
    patch_count = counts[lax.axis_index("narrow"), 0]
    indices = obs_index[0, 0]
    obs_values = obs_value[0, 0]
    weight_tile = obs_weight[0, 0]
    observed = jnp.take(anomaly, indices, axis=1)
    obs_mean = jnp.take(member_mean, indices, axis=0)
    weight_float = weight_tile.astype(jnp.float32)
    weighted = (observed * weight_float[None]).astype(jnp.bfloat16)
    innovation = (weight_float * (obs_values - obs_mean)).astype(jnp.bfloat16)
    patch_weights = solve_slots(observed, weighted, innovation)
    result = combine_blocks(anomaly, member_mean, patch_weights, patch_count)
    return lax.all_to_all(result, "wide", split_axis=0, concat_axis=1, tiled=True)


def solution(mesh):
    return jax.shard_map(
        per_device,
        mesh=mesh,
        in_specs=(
            P("wide", "narrow"),
            P(None, "wide"),
            P("narrow", "wide", None, None),
            P("narrow", "wide", None, None),
            P("narrow", "wide", None, None),
        ),
        out_specs=P("wide", "narrow"),
        check_vma=False,
    )
```

profile of v0, /device:TPU:0, one launch (start us, length us, event | category | flops | bytes accessed | tf_op | source)
XLA Modules:
  0.0 103.1 jit_solution(5557484394621048334)
XLA Ops:
  0.0 1.9 %copy.56 = bf16[4,8,8,1024]{3,2,0,1:T(8,128)(2,1)} copy(bf16[4,8,8,1024]{3,2,1,0:T(8,128)(2,1)} %bitcast.109) | data formatting | bytes 1048576 | tf_op jit(solution)/shard_map/all_to_all | solution.py:74
  1.9 7.3 %all-to-all-start = ((bf16[32,8,1024]{2,0,1:T(8,128)(2,1)}), bf16[32,8,1024]{2,0,1:T(8,128)(2,1)S(1)}, u32[]{:S(2)}, u32[]{:S(2)}) async-start(bf16[32,8,1024]{2,0,1:T(8,128)(2,1)} %bitcast.102), calls=%async_computation | async-start | bytes 1048576 | tf_op jit(solution)/shard_map/all_to_all | solution.py:74
  9.2 0.6 constant_dynamic-slice_fusion
  9.8 1.2 %and_select_fusion = s32[8]{0:T(128)} fusion(s32[]{:T(128)} %bitcast.2), kind=kLoop, calls=%fused_computation.71 | loop fusion | flops 128 | bytes 36 | tf_op jit(solution)/shard_map/jit(floor_divide)/jit(_where)/select_n | solution.py:62
  11.1 0.7 fusion.15
  11.8 0.6 bitcast_convert_fusion
  12.4 11.3 %all-to-all-done = bf16[32,8,1024]{2,0,1:T(8,128)(2,1)S(1)} async-done(((bf16[32,8,1024]{2,0,1:T(8,128)(2,1)}), bf16[32,8,1024]{2,0,1:T(8,128)(2,1)S(1)}, u32[]{:S(2)}, u32[]{:S(2)}) %all-to-all-start) | async-done | bytes 524320 | tf_op jit(solution)/shard_map/all_to_all | solution.py:74
  23.8 16.7 %gather_fusion.1 = f32[4096]{0:T(1024)S(1)} fusion(f32[1024]{0:T(1024)S(1)} %get-tuple-element.8, s32[4096]{0:T(1024)S(1)} %broadcast_clamp_fusion), kind=kCustom, calls=%fused_computation.1 | custom fusion | bytes 49152 | tf_op jit(solution)/shard_map/jit(_take)/gather | solution.py:83
  40.5 0.6 reshape.129
  41.7 17.0 %gather_fusion = bf16[4096,256]{1,0:T(8,128)(2,1)} fusion(bf16[256,1024]{0,1:T(8,128)(2,1)S(1)} %subtract_convert_fusion.6, s32[4096]{0:T(1024)S(1)} %broadcast_clamp_fusion), kind=kCustom, calls=%fused_computation | custom fusion | bytes 4210688 | tf_op jit(solution)/shard_map/jit(_take)/gather | solution.py:82
  58.8 2.9 %copy.24 = bf16[8,512,256]{1,2,0:T(8,128)(2,1)S(1)} copy(bf16[8,512,256]{2,1,0:T(8,128)(2,1)} %bitcast.107) | data formatting | bytes 4194304 | tf_op jit(solution)/shard_map/jit(_take)/gather | solution.py:82
  61.7 0.9 fusion.21
  62.5 1.8 %multiply_reduce_fusion = (f32[8]{0:T(128)S(1)}, f32[8,256,256]{2,1,0:T(8,128)S(1)}) fusion(f32[256,256]{1,0:T(8,128)S(1)} %fusion.16, bf16[8,512,256]{1,2,0:T(8,128)(2,1)S(1)} %copy.24, pred[8,512]{1,0:T(8,128)(4,1)S(1)} %get-tuple-element.6, f32[8,512]{1,0:T(8,128)} %bitcast_convert_fusion), kind=kOutput, calls=%fused_computation.15 | convolution fusion | flops 543686656 | bytes 4476960 | tf_op jit(solution)/shard_map/ksn,lsn->skl/dot_general | solution.py:12
  64.4 0.5 multiply_sqrt_fusion
  64.9 0.7 divide_convert_fusion
  65.6 0.4 subtract_convert_fusion.5
  66.9 0.4 subtract_convert_fusion.4
  69.6 0.5 subtract_convert_fusion.2
  71.2 0.9 copy-done.2
  72.1 0.6 fusion.2
  72.8 0.5 subtract_convert_fusion.1
  73.2 1.0 copy-done.3
  74.7 0.5 copy-done.5
  75.2 3.0 %subtract_convert_fusion = bf16[8,256,256]{2,1,0:T(8,128)(2,1)} fusion(bf16[8,256,256]{2,1,0:T(8,128)(2,1)S(1)} %convolution_convert_fusion.3, bf16[8,256,256]{2,1,0:T(8,128)(2,1)S(1)} %convolution_convert_fusion.4, bf16[8,256,256]{2,1,0:T(8,128)(2,1)} %copy-done.3, f32[256,256]{1,0:T(8,128)S(1)} %copy-done.5), kind=kOutput, calls=%fused_computation.8 | convolution fusion | flops 538968064 | bytes 4456448 | tf_op jit(solution)/shard_map/skl,slm->skm/dot_general | solution.py:25
  78.2 1.7 %convolution_convert_fusion.1 = bf16[8,256,256]{2,1,0:T(8,128)(2,1)S(1)} fusion(bf16[8,256,256]{2,1,0:T(8,128)(2,1)} %subtract_convert_fusion, bf16[8,256,256]{2,1,0:T(8,128)(2,1)S(1)} %convolution_convert_fusion.3), kind=kOutput, calls=%fused_computation.19 | convolution fusion | flops 268959744 | bytes 3145728 | tf_op jit(solution)/shard_map/skl,slm->skm/dot_general | solution.py:32
  79.8 0.9 fusion.24
  80.8 0.9 fusion.22
  81.9 0.6 add_convert_fusion
  82.4 0.7 convolution_convert_fusion
  83.2 0.5 fusion.6
  84.2 18.1 %all_to_all.29 = bf16[8,32,1024]{2,1,0:T(8,128)(2,1)S(1)} all-to-all(bf16[8,32,1024]{2,1,0:T(8,128)(2,1)S(1)} %convert_element_type.169), channel_id=1, replica_groups=mesh['wide'=8,'narrow'=4] {'wide'}, dimensions={0} | all-to-all | bytes 1048576 | tf_op jit(solution)/shard_map/all_to_all | solution.py:89
  102.3 0.8 copy.37
  (44 shorter events, 6.1 us)
Async XLA Ops:
  0.0 9.2 %copy-start = (s32[4,1]{0,1:T(1,128)S(1)}, s32[4,1]{0,1:T(1,128)}, u32[]{:S(2)}) copy-start(s32[4,1]{0,1:T(1,128)} %param.6) | copy-start | bytes 52
  0.0 9.2 %copy-start.6 = (s32[1,1,8,512]{3,2,1,0:T(8,128)S(1)}, s32[1,1,8,512]{3,2,1,0:T(8,128)}, u32[]{:S(2)}) copy-start(s32[1,1,8,512]{3,2,1,0:T(8,128)} %param.7) | copy-start | bytes 49156
  0.0 11.8 %copy-start.7 = (bf16[1,1,8,512]{3,2,1,0:T(8,128)(2,1)S(1)}, bf16[1,1,8,512]{3,2,1,0:T(8,128)(2,1)}, u32[]{:S(2)}) copy-start(bf16[1,1,8,512]{3,2,1,0:T(8,128)(2,1)} %param.9) | copy-start | bytes 24580
  1.9 21.8 %all-to-all-start = ((bf16[32,8,1024]{2,0,1:T(8,128)(2,1)}), bf16[32,8,1024]{2,0,1:T(8,128)(2,1)S(1)}, u32[]{:S(2)}, u32[]{:S(2)}) async-start(bf16[32,8,1024]{2,0,1:T(8,128)(2,1)} %bitcast.102), calls=%async_computation | async-start | bytes 1048576 | tf_op jit(solution)/shard_map/all_to_all | solution.py:74
  61.6 2.7 %copy-start.1 = (bf16[8,512,256]{1,2,0:T(8,128)(2,1)}, bf16[8,512,256]{1,2,0:T(8,128)(2,1)S(1)}, u32[]{:S(2)}) copy-start(bf16[8,512,256]{1,2,0:T(8,128)(2,1)S(1)} %copy.24) | copy-start | bytes 6291460
  64.4 1.2 %copy-start.4 = (f32[256,256]{1,0:T(8,128)S(1)}, f32[256,256]{1,0:T(8,128)}, u32[]{:S(2)}) copy-start(f32[256,256]{1,0:T(8,128)} %fusion.15) | copy-start | bytes 786436
  70.5 1.6 %copy-start.2 = (bf16[8,512,256]{1,2,0:T(8,128)(2,1)S(1)}, bf16[8,512,256]{1,2,0:T(8,128)(2,1)}, u32[]{:S(2)}) copy-start(bf16[8,512,256]{1,2,0:T(8,128)(2,1)} %copy-done.1) | copy-start | bytes 6291460
  73.2 1.0 copy-start.3
  74.2 0.9 copy-start.5
  79.8 2.0 %copy-start.9 = (f32[8]{0:T(128)S(1)}, f32[8]{0:T(128)}, u32[]{:S(2)}) copy-start(f32[8]{0:T(128)} %get-tuple-element.9) | copy-start | bytes 100
  81.7 0.7 copy-start.8
where the time goes:
time: 104 us; the launch traced here: 103 us
  local copies, waits for them, and re-layouts  44 us (42%)
  blocking collectives  18.1 us (17%)
  matrix products  16.4 us (16%)
  waiting for transfers between devices  11.3 us (11%)
  starting transfers between devices  7.28 us (7%)
  other arithmetic  5.74 us (6%)
    gather x2, local copies, waits for them, and re-layouts, per_device(): observed = jnp.take(anomaly, indices, axis=1)  19.9 us
    all_to_all x1, blocking collectives, per_device(): lax.all_to_all(result, 'wide', split_axis=0, concat_axis=1, tiled=True)  18.1 us
    gather x2, local copies, waits for them, and re-layouts, per_device(): obs_mean = jnp.take(member_mean, indices, axis=0)  17.3 us
    all_to_all x1, waiting for transfers between devices, per_device(): lax.all_to_all(fields, 'wide', split_axis=1, concat_axis=0, tiled=True)  11.3 us
    all_to_all x1, starting transfers between devices, per_device(): lax.all_to_all(fields, 'wide', split_axis=1, concat_axis=0, tiled=True)  7.28 us
    dot_general x6, matrix products, newton_steps(): jnp.einsum('skl,slm->skm', root_matrix, iterate, preferred_element_type=j...  5.27 us
    dot_general x6, matrix products, newton_steps(): jnp.einsum('skl,slm->skm', factor, root_matrix, preferred_element_type=jn...  3.85 us
    unnamed x22, local copies, waits for them, and re-layouts  2.64 us
  transfers between devices with their start and end apart: 1, of which 1 were waited for; matrix products, arithmetic and copies ran while one was open for 3% of the time, Pallas kernels for 0%

commit v1 on v0

v1 whole, which is shorter than its diff:
```python
import functools

import jax
import jax.numpy as jnp
from jax import lax
from jax.experimental import pallas as pl
from jax.experimental.pallas import tpu as pltpu
from jax.sharding import PartitionSpec as P

NS_ITERS = 6
MEAN_ROWS = 16
F32 = jnp.float32
BF16 = jnp.bfloat16


def dot(left, right, contract=((1,), (0,))):
    return lax.dot_general(left, right, (contract, ((), ())), preferred_element_type=F32)


def newton_steps(iterates, eye):
    roots = [None] * len(iterates)
    for step in range(NS_ITERS):
        products = iterates if step == 0 else [dot(r, y) for r, y in zip(roots, iterates)]
        factors = [(1.5 * eye - 0.5 * p.astype(F32)).astype(BF16) for p in products]
        if step < NS_ITERS - 1:
            iterates = [dot(y, f).astype(BF16) for y, f in zip(iterates, factors)]
        roots = factors if step == 0 else [dot(f, r).astype(BF16) for f, r in zip(factors, roots)]
    return roots


def analysis_kernel(count_ref, x_ref, index_ref, value_ref, weight_ref, out_ref, anomaly_s, mean_s, weight_s, pick_s):
    members, cells = x_ref.shape
    slots, nobs = index_ref.shape
    width = cells // slots
    x = x_ref[...].astype(F32)
    mean = jnp.sum(x, axis=0, keepdims=True) / members
    anomaly_s[:members, :] = (x - mean).astype(BF16)
    high = mean.astype(BF16).astype(F32)
    middle = (mean - high).astype(BF16).astype(F32)
    low = mean - high - middle
    row = lax.broadcasted_iota(jnp.int32, (MEAN_ROWS, cells), 0)
    parts = jnp.where(row == 0, high, jnp.where(row == 1, middle, jnp.where(row == 2, low, 0.0)))
    anomaly_s[members:, :] = parts.astype(BF16)
    for j in range(slots):
        mean_s[j : j + 1, :] = mean[:, j * width : (j + 1) * width]
    weight_s[...] = weight_ref[...].astype(F32)
    count = count_ref[0]
    square = (members, members)
    eye = (lax.broadcasted_iota(jnp.int32, square, 0) == lax.broadcasted_iota(jnp.int32, square, 1)).astype(F32)
    cell_ids = lax.broadcasted_iota(jnp.int32, (width, nobs), 0)
    lane = lax.broadcasted_iota(jnp.int32, (members, width), 1)
    iterates, scales, rights = [], [], []
    for block in range(slots):
        slot = (block * count) // slots
        index = index_ref[pl.ds(slot, 1), :]
        weight = weight_s[pl.ds(slot, 1), :]
        value = value_ref[pl.ds(slot, 1), :]
        within, part = lax.rem(index, width), lax.div(index, width)
        one_hot = (cell_ids == within).astype(F32).astype(BF16)
        for j in range(slots):
            pick_s[block, j * width : (j + 1) * width, :] = one_hot * (part == j).astype(F32).astype(BF16)
        picked = dot(anomaly_s[...], pick_s[block])
        observed = picked[:members]
        obs_mean = picked[members : members + 1] + picked[members + 1 : members + 2] + picked[members + 2 : members + 3]
        innovation = (weight * (value - obs_mean)).astype(BF16).astype(F32)
        weighted = (observed * weight).astype(BF16)
        rights.append(jnp.sum(observed * innovation, axis=1, keepdims=True))
        gram = dot(weighted, observed.astype(BF16), ((1,), (1,))) + (members - 1.0) * eye
        scale = jnp.sqrt(jnp.sum(jnp.sum(gram * gram, axis=0, keepdims=True), axis=1, keepdims=True))
        scales.append(scale)
        iterates.append((gram * (1.0 / scale)).astype(BF16))
    roots = newton_steps(iterates, eye)
    for block in range(slots):
        cols = slice(block * width, (block + 1) * width)
        root, right, scale = roots[block], rights[block], scales[block]
        high = right.astype(BF16).astype(F32)
        columns = jnp.where(lane == 0, high, jnp.where(lane == 1, right - high, 0.0)).astype(BF16)
        inner = dot(root, columns)
        inner = inner[:, 0:1] + inner[:, 1:2]
        moved = dot(root, anomaly_s[:members, cols], ((0,), (0,)))
        shift = jnp.sum(moved * inner, axis=0, keepdims=True) / scale + mean_s[block : block + 1, :]
        out_ref[:, cols] = (jnp.sqrt((members - 1.0) / scale) * moved + shift).astype(BF16)


def analyse(tile_fields, count, index, value, weight):
    members, cells = tile_fields.shape
    slots, nobs = index.shape
    vmem = pl.BlockSpec(memory_space=pltpu.VMEM)
    return pl.pallas_call(
        analysis_kernel,
        out_shape=jax.ShapeDtypeStruct((members, cells), BF16),
        in_specs=[pl.BlockSpec(memory_space=pltpu.SMEM)] + [vmem] * 4,
        out_specs=vmem,
        scratch_shapes=[
            pltpu.VMEM((members + MEAN_ROWS, cells), BF16),
            pltpu.VMEM((slots, cells // slots), F32),
            pltpu.VMEM((slots, nobs), F32),
            pltpu.VMEM((slots, cells, nobs), BF16),
        ],
        compiler_params=pltpu.CompilerParams(vmem_limit_bytes=48 << 20),
    )(count, tile_fields, index, value, weight)


def per_device(fields, counts, obs_index, obs_value, obs_weight):
    tile_fields = lax.all_to_all(fields, "wide", split_axis=1, concat_axis=0, tiled=True)
    count = lax.dynamic_slice(counts[:, 0], (lax.axis_index("narrow"),), (1,))
    result = analyse(tile_fields, count, obs_index[0, 0], obs_value[0, 0], obs_weight[0, 0])
    return lax.all_to_all(result, "wide", split_axis=0, concat_axis=1, tiled=True)


def solution(mesh):
    return jax.shard_map(
        per_device,
        mesh=mesh,
        in_specs=(
            P("wide", "narrow"),
            P(None, "wide"),
            P("narrow", "wide", None, None),
            P("narrow", "wide", None, None),
            P("narrow", "wide", None, None),
        ),
        out_specs=P("wide", "narrow"),
        check_vma=False,
    )
```

time: 104 us -> 53 us (0.51)
  local copies, waits for them, and re-layouts: 44 us -> 3.31 us
  matrix products: 16.4 us -> 0 us
  Pallas kernels: 0 us -> 9.92 us
  other arithmetic: 5.74 us -> 0 us
  waiting for transfers between devices: 11.3 us -> 13.9 us
    gather x4 -> x0, local copies, waits for them, and re-layouts: 37.2 us -> none  [the longest x2 19.9 us: per_device(): observed = jnp.take(anomaly, indices, axis=1)]
    dot_general x22 -> x0, matrix products: 16.4 us -> none  [the longest x6 5.27 us: newton_steps(): jnp.einsum('skl,slm->skm', root_matrix, iterate, preferred_element_type=j...]
    pallas_call x0 -> x1, Pallas kernels: none -> 9.92 us  [analyse(): pl.pallas_call(analysis_kernel, out_shape=jax.ShapeDtypeStruct((members,...]
    convert_element_type x8 -> x0, other arithmetic: 3.1 us -> none  [the longest x1 0.88 us: per_device(): innovation = (weight_float * (obs_values - obs_mean)).astype(jnp.bfloat16)]
    all_to_all x1, waiting for transfers between devices: 11.3 us -> 13.9 us  [per_device(): lax.all_to_all(fields, 'wide', split_axis=1, concat_axis=0, tiled=True)]
    unnamed x22 -> x8, local copies, waits for them, and re-layouts: 2.64 us -> 0.02 us
    select_n x1 -> x0, other arithmetic: 1.18 us -> none  [combine_blocks(): owner_patch = block_ids * patch_count // slot_total]
  transfers between devices with their start and end apart: 1 -> 1, of which waited for: 1 -> 1; matrix products, arithmetic and copies ran while one was open for 3% -> 1% of each run, Pallas kernels for 0% -> 0%
where the time goes in v1:
time: 53 us; the launch traced here: 52.7 us
  blocking collectives  18.1 us (34%)
  waiting for transfers between devices  13.9 us (26%)
  Pallas kernels  9.92 us (19%)
  starting transfers between devices  7.41 us (14%)
  local copies, waits for them, and re-layouts  3.31 us (6%)
    all_to_all x1, blocking collectives, per_device(): lax.all_to_all(result, 'wide', split_axis=0, concat_axis=1, tiled=True)  18.1 us
    all_to_all x1, waiting for transfers between devices, per_device(): lax.all_to_all(fields, 'wide', split_axis=1, concat_axis=0, tiled=True)  13.9 us
    pallas_call x1, Pallas kernels, analyse(): pl.pallas_call(analysis_kernel, out_shape=jax.ShapeDtypeStruct((members,...  9.92 us
    all_to_all x1, starting transfers between devices, per_device(): lax.all_to_all(fields, 'wide', split_axis=1, concat_axis=0, tiled=True)  7.41 us
    all_to_all x1, local copies, waits for them, and re-layouts, per_device(): lax.all_to_all(fields, 'wide', split_axis=1, concat_axis=0, tiled=True)  1.89 us
  transfers between devices with their start and end apart: 1, of which 1 were waited for; matrix products, arithmetic and copies ran while one was open for 1% of the time, Pallas kernels for 0%

profile of v1, /device:TPU:0, one launch (start us, length us, event | category | flops | bytes accessed | tf_op | source)
XLA Modules:
  0.0 52.7 jit_solution(13498638838169698702)
XLA Ops:
  0.0 0.0 copy-start
  0.0 1.9 %copy.11 = bf16[4,8,8,1024]{3,2,0,1:T(8,128)(2,1)} copy(bf16[4,8,8,1024]{3,2,1,0:T(8,128)(2,1)} %bitcast.21) | data formatting | bytes 1048576 | tf_op jit(solution)/shard_map/all_to_all | solution.py:105
  1.9 0.0 copy-start.2
  1.9 0.0 copy-start.3
  1.9 7.4 %all-to-all-start = ((bf16[32,8,1024]{2,0,1:T(8,128)(2,1)}), bf16[32,8,1024]{2,0,1:T(8,128)(2,1)S(1)}, u32[]{:S(2)}, u32[]{:S(2)}) async-start(bf16[32,8,1024]{2,0,1:T(8,128)(2,1)} %bitcast.14), calls=%async_computation | async-start | bytes 1048576 | tf_op jit(solution)/shard_map/all_to_all | solution.py:105
  9.3 0.0 copy-start.1
  9.3 0.0 copy-done
  9.3 0.6 %constant_dynamic-slice_fusion = s32[1,1]{0,1:T(1,128)} fusion(s32[4,1]{0,1:T(1,128)S(1)} %copy-done, s32[]{:T(128)S(6)} %select_n.3), kind=kLoop, calls=%fused_computation.1 | loop fusion | bytes 12 | tf_op jit(solution)/shard_map/dynamic_slice | solution.py:106
  9.9 13.9 %all-to-all-done = bf16[32,8,1024]{2,0,1:T(8,128)(2,1)S(1)} async-done(((bf16[32,8,1024]{2,0,1:T(8,128)(2,1)}), bf16[32,8,1024]{2,0,1:T(8,128)(2,1)S(1)}, u32[]{:S(2)}, u32[]{:S(2)}) %all-to-all-start) | async-done | bytes 524320 | tf_op jit(solution)/shard_map/all_to_all | solution.py:105
  23.8 0.0 copy-done.2
  23.8 0.0 copy-done.3
  23.8 0.0 copy-done.1
  23.8 9.9 %shard_map.55 = bf16[256,1024]{1,0:T(8,128)(2,1)S(1)} custom-call(s32[1]{0:T(128)} %bitcast.count_ref, bf16[256,1024]{1,0:T(8,128)(2,1)S(1)} %bitcast.15, s32[8,512]{1,0:T(8,128)S(1)} %bitcast.17, f32[8,512]{1,0:T(8,128)S(1)} %bitcast.18, bf16[8,512]{1,0:T(8,128)(2,1)S(1)} %bitcast.19), custom_call_target="tpu_custom_call" | custom-call | tf_op jit(solution)/shard_map/pallas_call | solution.py:89
  33.7 18.1 %all_to_all.38 = bf16[8,32,1024]{2,1,0:T(8,128)(2,1)S(1)} all-to-all(bf16[8,32,1024]{2,1,0:T(8,128)(2,1)S(1)} %bitcast.16), channel_id=1, replica_groups=mesh['wide'=8,'narrow'=4] {'wide'}, dimensions={0} | all-to-all | bytes 1048576 | tf_op jit(solution)/shard_map/all_to_all | solution.py:108
  51.8 0.8 %copy.9 = bf16[8,4,8,1024]{3,2,0,1:T(8,128)(2,1)} copy(bf16[8,4,8,1024]{3,2,1,0:T(8,128)(2,1)S(1)} %bitcast.20) | data formatting | bytes 1048576 | tf_op jit(solution)/shard_map/all_to_all | solution.py:108
Async XLA Ops:
  0.0 9.3 %copy-start = (s32[4,1]{0,1:T(1,128)S(1)}, s32[4,1]{0,1:T(1,128)}, u32[]{:S(2)}) copy-start(s32[4,1]{0,1:T(1,128)} %param.6) | copy-start | bytes 52
  1.9 21.9 %copy-start.2 = (f32[1,1,8,512]{3,2,1,0:T(8,128)S(1)}, f32[1,1,8,512]{3,2,1,0:T(8,128)}, u32[]{:S(2)}) copy-start(f32[1,1,8,512]{3,2,1,0:T(8,128)} %param.8) | copy-start | bytes 49156
  1.9 21.9 %copy-start.3 = (bf16[1,1,8,512]{3,2,1,0:T(8,128)(2,1)S(1)}, bf16[1,1,8,512]{3,2,1,0:T(8,128)(2,1)}, u32[]{:S(2)}) copy-start(bf16[1,1,8,512]{3,2,1,0:T(8,128)(2,1)} %param.9) | copy-start | bytes 24580
  1.9 21.9 %all-to-all-start = ((bf16[32,8,1024]{2,0,1:T(8,128)(2,1)}), bf16[32,8,1024]{2,0,1:T(8,128)(2,1)S(1)}, u32[]{:S(2)}, u32[]{:S(2)}) async-start(bf16[32,8,1024]{2,0,1:T(8,128)(2,1)} %bitcast.14), calls=%async_computation | async-start | bytes 1048576 | tf_op jit(solution)/shard_map/all_to_all | solution.py:105
  9.3 14.5 %copy-start.1 = (s32[1,1,8,512]{3,2,1,0:T(8,128)S(1)}, s32[1,1,8,512]{3,2,1,0:T(8,128)}, u32[]{:S(2)}) copy-start(s32[1,1,8,512]{3,2,1,0:T(8,128)} %param.7) | copy-start | bytes 49156

commit v2 on v1

v2 whole, which is shorter than its diff:
```python
import functools

import jax
import jax.numpy as jnp
from jax import lax
from jax.experimental import pallas as pl
from jax.experimental.pallas import tpu as pltpu
from jax.sharding import PartitionSpec as P


NS_ITERS = 6
PARTNERS = (6, 5, 3, 7, 2, 4, 1)
PACKED_ROWS = 16
F32 = jnp.float32
BF16 = jnp.bfloat16
VMEM = pl.BlockSpec(memory_space=pltpu.VMEM)
SMEM = pl.BlockSpec(memory_space=pltpu.SMEM)


def dot(left, right, contract=((1,), (0,))):
    return lax.dot_general(left, right, (contract, ((), ())), preferred_element_type=F32)


def pick_rows(rows, index, pick_s, slots):
    cells, nobs = pick_s.shape
    width = cells // slots
    cell_ids = lax.broadcasted_iota(jnp.int32, (width, nobs), 0)
    within, part = lax.rem(index, width), lax.div(index, width)
    one_hot = (cell_ids == within).astype(F32).astype(BF16)
    for j in range(slots):
        pick_s[j * width : (j + 1) * width, :] = one_hot * (part == j).astype(F32).astype(BF16)
    return dot(rows, pick_s[...])


def early_kernel(parts, count_ref, index_ref, value_ref, weight_ref, *refs):
    chunk_refs = refs[:parts]
    picked_ref, total_ref, index_out, value_out, weight_out, weight_s, pick_s = refs[parts:]
    slots, nobs = index_ref.shape
    count = count_ref[0]
    weight_s[...] = weight_ref[...].astype(F32)
    rows = jnp.concatenate([ref[...] for ref in chunk_refs], axis=0)
    for block in range(slots):
        slot = (block * count) // slots
        index = index_ref[pl.ds(slot, 1), :]
        index_out[block : block + 1, :] = index
        value_out[block : block + 1, :] = value_ref[pl.ds(slot, 1), :]
        weight_out[block : block + 1, :] = weight_s[pl.ds(slot, 1), :]
        picked = pick_rows(rows, index, pick_s.at[block % 2], slots)
        total_ref[block : block + 1, :] = jnp.sum(picked, axis=0, keepdims=True)
        picked_ref[:, block * nobs : (block + 1) * nobs] = picked.astype(BF16)


def newton_steps(iterates, eye):
    roots = [None] * len(iterates)
    for step in range(NS_ITERS):
        products = iterates if step == 0 else [dot(r, y) for r, y in zip(roots, iterates)]
        factors = [(1.5 * eye - 0.5 * p.astype(F32)).astype(BF16) for p in products]
        if step < NS_ITERS - 1:
            iterates = [dot(y, f).astype(BF16) for y, f in zip(iterates, factors)]
        roots = factors if step == 0 else [dot(f, r).astype(BF16) for f, r in zip(factors, roots)]
    return roots


def main_kernel(parts, early, index_ref, value_ref, weight_ref, picked_ref, total_ref, *refs):
    chunk_refs, out_refs = refs[:parts], refs[parts : 2 * parts]
    anomaly_s, mean_s, pick_s = refs[2 * parts :]
    share, cells = chunk_refs[0].shape
    members = share * parts
    slots, nobs = index_ref.shape
    width = cells // slots
    total = sum(jnp.sum(ref[...].astype(F32), axis=0, keepdims=True) for ref in chunk_refs)
    mean = total / members
    for p, ref in enumerate(chunk_refs):
        anomaly_s[p * share : (p + 1) * share, :] = (ref[...].astype(F32) - mean).astype(BF16)
    for j in range(slots):
        mean_s[j : j + 1, :] = mean[:, j * width : (j + 1) * width]
    square = (members, members)
    eye = (lax.broadcasted_iota(jnp.int32, square, 0) == lax.broadcasted_iota(jnp.int32, square, 1)).astype(F32)
    late = jnp.concatenate([ref[...] for ref in chunk_refs[early:]], axis=0)
    extra = lax.broadcasted_iota(jnp.int32, (PACKED_ROWS, nobs), 0) == 0
    iterates, scales, rights = [], [], []
    for block in range(slots):
        line = slice(block, block + 1)
        weight = weight_ref[line, :]
        picked = pick_rows(late, index_ref[line, :], pick_s.at[block % 2], slots)
        obs_mean = (total_ref[line, :] + jnp.sum(picked, axis=0, keepdims=True)) / members
        innovation = weight * (value_ref[line, :] - obs_mean)
        before = picked_ref[:, block * nobs : (block + 1) * nobs].astype(F32)
        observed = jnp.concatenate([(before - obs_mean).astype(BF16), (picked - obs_mean).astype(BF16)], axis=0)
        weighted = (observed.astype(F32) * weight).astype(BF16)
        left = jnp.concatenate([weighted, jnp.where(extra, innovation, 0.0).astype(BF16)], axis=0)
        products = dot(left, observed, ((1,), (1,)))
        rights.append(products[members : members + 1])
        gram = products[:members] + (members - 1.0) * eye
        scale = jnp.sqrt(jnp.sum(jnp.sum(gram * gram, axis=0, keepdims=True), axis=1, keepdims=True))
        scales.append(scale)
        iterates.append((gram * (1.0 / scale)).astype(BF16))
    roots = newton_steps(iterates, eye)
    for block in range(slots):
        cols = slice(block * width, (block + 1) * width)
        root, right, scale = roots[block], rights[block], scales[block]
        inner = jnp.sum(root.astype(F32) * right, axis=1, keepdims=True)
        moved = dot(root, anomaly_s[:, cols], ((0,), (0,)))
        shift = jnp.sum(moved * inner, axis=0, keepdims=True) / scale + mean_s[block : block + 1, :]
        result = (jnp.sqrt((members - 1.0) / scale) * moved + shift).astype(BF16)
        for p, ref in enumerate(out_refs):
            ref[:, cols] = result[p * share : (p + 1) * share]


def analyse(chunks, early, count, index, value, weight):
    parts = len(chunks)
    share, cells = chunks[0].shape
    slots, nobs = index.shape
    line = jax.ShapeDtypeStruct((slots, nobs), F32)
    rows = share * early
    picked, total, index, value, weight = pl.pallas_call(
        functools.partial(early_kernel, early),
        out_shape=[
            jax.ShapeDtypeStruct((rows, slots * nobs), BF16),
            line,
            jax.ShapeDtypeStruct((slots, nobs), jnp.int32),
            line,
            line,
        ],
        in_specs=[SMEM] + [VMEM] * (3 + early),
        out_specs=[VMEM] * 5,
        scratch_shapes=[pltpu.VMEM((slots, nobs), F32), pltpu.VMEM((2, cells, nobs), BF16)],
        cost_estimate=pl.CostEstimate(
            flops=2 * rows * cells * slots * nobs, bytes_accessed=rows * slots * nobs * 2, transcendentals=0
        ),
        compiler_params=pltpu.CompilerParams(vmem_limit_bytes=16 << 20),
    )(count, index, value, weight, *chunks[:early])
    return pl.pallas_call(
        functools.partial(main_kernel, parts, early),
        out_shape=[jax.ShapeDtypeStruct((share, cells), BF16)] * parts,
        in_specs=[VMEM] * (5 + parts),
        out_specs=[VMEM] * parts,
        scratch_shapes=[
            pltpu.VMEM((share * parts, cells), BF16),
            pltpu.VMEM((slots, cells // slots), F32),
            pltpu.VMEM((2, cells, nobs), BF16),
        ],
        compiler_params=pltpu.CompilerParams(vmem_limit_bytes=40 << 20),
    )(index, value, weight, picked, total, *chunks)


def partner_order(parts):
    return tuple(s for s in PARTNERS if s < parts) + tuple(range(len(PARTNERS) + 1, parts))


def by_permutes(parts, share):
    return parts & (parts - 1) == 0 and share % PACKED_ROWS == 0


def exchange(block, step):
    return lax.ppermute(block, "wide", [(i, i ^ step) for i in range(lax.axis_size("wide"))])


def per_device(fields, counts, obs_index, obs_value, obs_weight):
    parts, me = lax.axis_size("wide"), lax.axis_index("wide")
    share, width = fields.shape
    cells = width // parts
    count = lax.dynamic_slice(counts[:, 0], (lax.axis_index("narrow"),), (1,))
    tile = (count, obs_index[0, 0], obs_value[0, 0], obs_weight[0, 0])
    if not by_permutes(parts, share):
        whole = lax.all_to_all(fields, "wide", split_axis=1, concat_axis=0, tiled=True)
        half = whole.shape[0] // 2
        result = jnp.concatenate(analyse([whole[:half], whole[half:]], 1, *tile), axis=0)
        return lax.all_to_all(result, "wide", split_axis=0, concat_axis=1, tiled=True)
    order = partner_order(parts)
    steps = (0,) + order
    blocks = [lax.dynamic_slice(fields, (0, (me ^ s) * cells), (share, cells)) for s in steps]
    chunks = [blocks[0]] + [exchange(b, s) for b, s in zip(blocks[1:], order)]
    results = analyse(chunks, parts // 2, *tile)
    returned = [results[0]] + [exchange(b, s) for b, s in zip(results[1:], order)]
    analysis = jnp.zeros_like(fields)
    for s, block in zip(steps, returned):
        analysis = lax.dynamic_update_slice(analysis, block, (0, (me ^ s) * cells))
    return analysis


def solution(mesh):
    return jax.shard_map(
        per_device,
        mesh=mesh,
        in_specs=(
            P("wide", "narrow"),
            P(None, "wide"),
            P("narrow", "wide", None, None),
            P("narrow", "wide", None, None),
            P("narrow", "wide", None, None),
        ),
        out_specs=P("wide", "narrow"),
        check_vma=False,
    )
```

time: 53 us -> 42.8 us (0.81)
  blocking collectives: 18.1 us -> 0 us
  starting transfers between devices: 7.41 us -> 24.9 us
  waiting for transfers between devices: 13.9 us -> 4.29 us
  Pallas kernels: 9.92 us -> 10.8 us
  local copies, waits for them, and re-layouts: 3.31 us -> 2.47 us
    ppermute x0 -> x14, starting transfers between devices: none -> 24.9 us  [exchange(): lax.ppermute(block, 'wide', [(i, i ^ step) for i in range(lax.axis_size('...]
    all_to_all x1 -> x0, blocking collectives: 18.1 us -> none  [per_device(): lax.all_to_all(result, 'wide', split_axis=0, concat_axis=1, tiled=True)]
    all_to_all x1 -> x0, waiting for transfers between devices: 13.9 us -> none  [per_device(): lax.all_to_all(fields, 'wide', split_axis=1, concat_axis=0, tiled=True)]
    all_to_all x1 -> x0, starting transfers between devices: 7.41 us -> none  [per_device(): lax.all_to_all(fields, 'wide', split_axis=1, concat_axis=0, tiled=True)]
    ppermute x0 -> x14, waiting for transfers between devices: none -> 4.29 us  [exchange(): lax.ppermute(block, 'wide', [(i, i ^ step) for i in range(lax.axis_size('...]
    all_to_all x2 -> x0, local copies, waits for them, and re-layouts: 2.72 us -> none  [the longest x1 1.89 us: per_device(): lax.all_to_all(fields, 'wide', split_axis=1, concat_axis=0, tiled=True)]
    dynamic_slice x0 -> x1, local copies, waits for them, and re-layouts: none -> 1.12 us  [per_device(): lax.dynamic_slice(fields, (0, (me ^ s) * cells), (share, cells))]
    pallas_call x1 -> x2, Pallas kernels: 9.92 us -> 10.8 us  [the longest x1 8.76 us: analyse(): pl.pallas_call(functools.partial(main_kernel, parts, early), out_shape=[j...]
  transfers between devices with their start and end apart: 1 -> 14, of which waited for: 1 -> 5; matrix products, arithmetic and copies ran while one was open for 1% -> 2% of each run, Pallas kernels for 0% -> 5%
where the time goes in v2:
time: 42.8 us; the launch traced here: 42.6 us
  starting transfers between devices  24.9 us (58%)
  Pallas kernels  10.8 us (25%)
  waiting for transfers between devices  4.29 us (10%)
  local copies, waits for them, and re-layouts  2.47 us (6%)
    ppermute x14, starting transfers between devices, exchange(): lax.ppermute(block, 'wide', [(i, i ^ step) for i in range(lax.axis_size('...  24.9 us
    pallas_call x1, Pallas kernels, analyse(): pl.pallas_call(functools.partial(main_kernel, parts, early), out_shape=[j...  8.76 us
    ppermute x14, waiting for transfers between devices, exchange(): lax.ppermute(block, 'wide', [(i, i ^ step) for i in range(lax.axis_size('...  4.29 us
    pallas_call x1, Pallas kernels, analyse(): pl.pallas_call(functools.partial(early_kernel, early), out_shape=[jax.Sha...  2.02 us
    dynamic_slice x1, local copies, waits for them, and re-layouts, per_device(): lax.dynamic_slice(fields, (0, (me ^ s) * cells), (share, cells))  1.12 us
  transfers between devices with their start and end apart: 14, of which 5 were waited for; matrix products, arithmetic and copies ran while one was open for 2% of the time, Pallas kernels for 5%

profile of v2, /device:TPU:0, one launch (start us, length us, event | category | flops | bytes accessed | tf_op | source)
XLA Modules:
  0.0 42.6 jit_solution(1921937944599572400)
XLA Ops:
  0.0 1.1 %constant_dynamic-slice_fusion = (bf16[32,1024]{1,0:T(8,128)(2,1)S(1)}, bf16[32,1024]{1,0:T(8,128)(2,1)S(1)}, bf16[32,1024]{1,0:T(8,128)(2,1)S(1)}, bf16[32,1024...) fusion(bf16[32,8192]{1,0:T(8,128)(2,1)} %param.5, ...), kind=kLoop, calls=%fused_computation.8 | loop fusion | bytes 1048608 | tf_op jit(solution)/shard_map/dynamic_slice | solution.py:172
  1.1 0.0 copy-start.1
  1.1 0.0 copy-start.2
  1.2 5.1 %collective-permute-start = (bf16[32,1024]{1,0:T(8,128)(2,1)S(1)}, bf16[32,1024]{1,0:T(8,128)(2,1)S(1)}, u32[]{:S(2)}, u32[]{:S(2)}) collective-permute-start(bf16[32,1024]{1,0:T(8,128)(2,1)S(1)} %get-tuple-element.36), channel_id=1, source_target_pairs={{0,24},{4,28},{8,16},{12,20},{16,8},{20,12},{24,0},{28,4},{1,25},{... | collective-permute-start | bytes 196616 | tf_op jit(solution)/shard_map/ppermute | solution.py:156
  6.3 0.4 collective-permute-start.1
  6.7 1.2 %collective-permute-start.2 = (bf16[32,1024]{1,0:T(8,128)(2,1)S(1)}, bf16[32,1024]{1,0:T(8,128)(2,1)S(1)}, u32[]{:S(2)}, u32[]{:S(2)}) collective-permute-start(bf16[32,1024]{1,0:T(8,128)(2,1)S(1)} %get-tuple-element.34), channel_id=1, source_target_pairs={{0,12},{4,8},{8,4},{12,0},{16,28},{20,24},{24,20},{28,16},{1,13},{... | collective-permute-start | bytes 196616 | tf_op jit(solution)/shard_map/ppermute | solution.py:156
  7.8 4.7 %collective-permute-start.3 = (bf16[32,1024]{1,0:T(8,128)(2,1)S(1)}, bf16[32,1024]{1,0:T(8,128)(2,1)S(1)}, u32[]{:S(2)}, u32[]{:S(2)}) collective-permute-start(bf16[32,1024]{1,0:T(8,128)(2,1)S(1)} %get-tuple-element.33), channel_id=1, source_target_pairs={{0,28},{4,24},{8,20},{12,16},{16,12},{20,8},{24,4},{28,0},{1,29},{... | collective-permute-start | bytes 196616 | tf_op jit(solution)/shard_map/ppermute | solution.py:156
  12.5 0.0 collective-permute-start.4
  12.5 0.6 %constant_dynamic-slice_fusion.8 = s32[1,1]{0,1:T(1,128)} fusion(s32[4,1]{0,1:T(1,128)S(1)} %copy-done, s32[]{:T(128)S(6)} %select_n.35), kind=kLoop, calls=%fused_computation.16 | loop fusion | bytes 12 | tf_op jit(solution)/shard_map/dynamic_slice | solution.py:163
  13.1 0.0 collective-permute-done.refs_1_
  13.1 0.8 %collective-permute-start.5 = (bf16[32,1024]{1,0:T(8,128)(2,1)S(1)}, bf16[32,1024]{1,0:T(8,128)(2,1)S(1)}, u32[]{:S(2)}, u32[]{:S(2)}) collective-permute-start(bf16[32,1024]{1,0:T(8,128)(2,1)S(1)} %get-tuple-element.38), channel_id=1, source_target_pairs={{0,16},{4,20},{8,24},{12,28},{16,0},{20,4},{24,8},{28,12},{1,17},{... | collective-permute-start | bytes 196616 | tf_op jit(solution)/shard_map/ppermute | solution.py:156
  13.9 0.0 collective-permute-done.1.refs_2_
  13.9 1.4 %collective-permute-start.6 = (bf16[32,1024]{1,0:T(8,128)(2,1)S(1)}, bf16[32,1024]{1,0:T(8,128)(2,1)S(1)}, u32[]{:S(2)}, u32[]{:S(2)}) collective-permute-start(bf16[32,1024]{1,0:T(8,128)(2,1)S(1)} %get-tuple-element.31), channel_id=1, source_target_pairs={{0,4},{4,0},{8,12},{12,8},{16,20},{20,16},{24,28},{28,24},{1,5},{5... | collective-permute-start | bytes 196616 | tf_op jit(solution)/shard_map/ppermute | solution.py:156
  15.3 2.0 %shard_map.55 = (bf16[128,4096]{1,0:T(8,128)(2,1)S(1)}, f32[8,512]{1,0:T(8,128)S(1)}, s32[8,512]{1,0:T(8,128)S(1)}, f32[8,512]{1,0:T(8,128)S(1)}, f32[8,512]{1,0:T(8,128)S(1)}) custom-call(s32[1]{0:T(128)} %bitcast.count_ref, s32[8,512]{1,0:T(8,128)S(1)} %bitcast.4, f32[8,512]{1,0:T(8,128)S(1)} %bitcast.5, bf16[8,512]{1,0:T(8,128)(2,1)S(1)} %bitcast.6, ...), custom_call_target="tpu_custom_call" | custom-call | flops 1073741824 | bytes 1048576 | tf_op jit(solution)/shard_map/pallas_call | solution.py:116
  17.3 0.0 collective-permute-done.3.refs_4_
  17.3 1.0 %collective-permute-done.5.refs_6_ = bf16[32,1024]{1,0:T(8,128)(2,1)S(1)} collective-permute-done((bf16[32,1024]{1,0:T(8,128)(2,1)S(1)}, bf16[32,1024]{1,0:T(8,128)(2,1)S(1)}, u32[]{:S(2)}, u32[]{:S(2)}) %collective-permute-start.5) | collective-permute-done | bytes 65568 | tf_op jit(solution)/shard_map/ppermute | solution.py:156
  18.3 8.8 %shard_map.56 = (bf16[32,1024]{1,0:T(8,128)(2,1)S(1)}, bf16[32,1024]{1,0:T(8,128)(2,1)S(1)}, bf16[32,1024]{1,0:T(8,128)(2,1)S(1)}, bf16[32,1024]{1,0:T(8,128)(2,...) custom-call(s32[8,512]{1,0:T(8,128)S(1)} %get-tuple-element.18.index, ...), custom_call_target="tpu_custom_call" | custom-call | tf_op jit(solution)/shard_map/pallas_call | solution.py:133
  27.0 3.6 %collective-permute-start.7 = (bf16[32,1024]{1,0:T(8,128)(2,1)S(1)}, bf16[32,1024]{1,0:T(8,128)(2,1)S(1)}, u32[]{:S(2)}, u32[]{:S(2)}) collective-permute-start(bf16[32,1024]{1,0:T(8,128)(2,1)S(1)} %get-tuple-element.24), channel_id=1, source_target_pairs={{0,24},{4,28},{8,16},{12,20},{16,8},{20,12},{24,0},{28,4},{1,25},{... | collective-permute-start | bytes 196616 | tf_op jit(solution)/shard_map/ppermute | solution.py:156
  30.6 0.0 collective-permute-start.8
  30.6 1.8 %collective-permute-start.9 = (bf16[32,1024]{1,0:T(8,128)(2,1)S(1)}, bf16[32,1024]{1,0:T(8,128)(2,1)S(1)}, u32[]{:S(2)}, u32[]{:S(2)}) collective-permute-start(bf16[32,1024]{1,0:T(8,128)(2,1)S(1)} %get-tuple-element.26), channel_id=1, source_target_pairs={{0,12},{4,8},{8,4},{12,0},{16,28},{20,24},{24,20},{28,16},{1,13},{... | collective-permute-start | bytes 196616 | tf_op jit(solution)/shard_map/ppermute | solution.py:156
  32.4 3.5 %collective-permute-start.10 = (bf16[32,1024]{1,0:T(8,128)(2,1)S(1)}, bf16[32,1024]{1,0:T(8,128)(2,1)S(1)}, u32[]{:S(2)}, u32[]{:S(2)}) collective-permute-start(bf16[32,1024]{1,0:T(8,128)(2,1)S(1)} %get-tuple-element.27), channel_id=1, source_target_pairs={{0,28},{4,24},{8,20},{12,16},{16,12},{20,8},{24,4},{28,0},{1,29},{... | collective-permute-start | bytes 196616 | tf_op jit(solution)/shard_map/ppermute | solution.py:156
  35.9 0.0 collective-permute-start.11
  35.9 1.7 %collective-permute-start.12 = (bf16[32,1024]{1,0:T(8,128)(2,1)S(1)}, bf16[32,1024]{1,0:T(8,128)(2,1)S(1)}, u32[]{:S(2)}, u32[]{:S(2)}) collective-permute-start(bf16[32,1024]{1,0:T(8,128)(2,1)S(1)} %get-tuple-element.29), channel_id=1, source_target_pairs={{0,16},{4,20},{8,24},{12,28},{16,0},{20,4},{24,8},{28,12},{1,17},{... | collective-permute-start | bytes 196616 | tf_op jit(solution)/shard_map/ppermute | solution.py:156
  37.6 0.0 collective-permute-done.8
  37.6 0.9 %collective-permute-start.13 = (bf16[32,1024]{1,0:T(8,128)(2,1)S(1)}, bf16[32,1024]{1,0:T(8,128)(2,1)S(1)}, u32[]{:S(2)}, u32[]{:S(2)}) collective-permute-start(bf16[32,1024]{1,0:T(8,128)(2,1)S(1)} %get-tuple-element.30), channel_id=1, source_target_pairs={{0,4},{4,0},{8,12},{12,8},{16,20},{20,16},{24,28},{28,24},{1,5},{5... | collective-permute-start | bytes 196616 | tf_op jit(solution)/shard_map/ppermute | solution.py:156
  38.6 0.0 collective-permute-done.9
  38.6 1.2 %collective-permute-done.10 = bf16[32,1024]{1,0:T(8,128)(2,1)S(1)} collective-permute-done((bf16[32,1024]{1,0:T(8,128)(2,1)S(1)}, bf16[32,1024]{1,0:T(8,128)(2,1)S(1)}, u32[]{:S(2)}, u32[]{:S(2)}) %collective-permute-start.10) | collective-permute-done | bytes 65568 | tf_op jit(solution)/shard_map/ppermute | solution.py:156
  39.9 0.6 %collective-permute-done.11 = bf16[32,1024]{1,0:T(8,128)(2,1)S(1)} collective-permute-done((bf16[32,1024]{1,0:T(8,128)(2,1)S(1)}, bf16[32,1024]{1,0:T(8,128)(2,1)S(1)}, u32[]{:S(2)}, u32[]{:S(2)}) %collective-permute-start.11) | collective-permute-done | bytes 65568 | tf_op jit(solution)/shard_map/ppermute | solution.py:156
  40.5 0.7 %collective-permute-done.12 = bf16[32,1024]{1,0:T(8,128)(2,1)S(1)} collective-permute-done((bf16[32,1024]{1,0:T(8,128)(2,1)S(1)}, bf16[32,1024]{1,0:T(8,128)(2,1)S(1)}, u32[]{:S(2)}, u32[]{:S(2)}) %collective-permute-start.12) | collective-permute-done | bytes 65568 | tf_op jit(solution)/shard_map/ppermute | solution.py:156
  41.2 0.0 copy-start.4
  41.2 0.8 %collective-permute-done.13 = bf16[32,1024]{1,0:T(8,128)(2,1)S(1)} collective-permute-done((bf16[32,1024]{1,0:T(8,128)(2,1)S(1)}, bf16[32,1024]{1,0:T(8,128)(2,1)S(1)}, u32[]{:S(2)}, u32[]{:S(2)}) %collective-permute-start.13) | collective-permute-done | bytes 65568 | tf_op jit(solution)/shard_map/ppermute | solution.py:156
  42.0 0.6 %constant_dynamic-update-slice_fusion = bf16[32,8192]{1,0:T(8,128)(2,1)} fusion(bf16[32,8192]{1,0:T(8,128)(2,1)} %copy-done.4, bf16[32,1024]{1,0:T(8,128)(2,1)S(1)} %collective-permute-done.13, s32[]{:T(128)S(6)} %select_n.43), kind=kLoop, calls=%fused_computation | loop fusion | bytes 131076 | tf_op jit(solution)/shard_map/dynamic_update_slice | solution.py:178
  (19 shorter events, 0.1 us)
Async XLA Ops:
  0.0 12.5 %copy-start = (s32[4,1]{0,1:T(1,128)S(1)}, s32[4,1]{0,1:T(1,128)}, u32[]{:S(2)}) copy-start(s32[4,1]{0,1:T(1,128)} %param.6) | copy-start | bytes 52
  0.0 15.3 %copy-start.3 = (bf16[1,1,8,512]{3,2,1,0:T(8,128)(2,1)S(1)}, bf16[1,1,8,512]{3,2,1,0:T(8,128)(2,1)}, u32[]{:S(2)}) copy-start(bf16[1,1,8,512]{3,2,1,0:T(8,128)(2,1)} %param.9) | copy-start | bytes 24580
  1.1 14.1 %copy-start.1 = (s32[1,1,8,512]{3,2,1,0:T(8,128)S(1)}, s32[1,1,8,512]{3,2,1,0:T(8,128)}, u32[]{:S(2)}) copy-start(s32[1,1,8,512]{3,2,1,0:T(8,128)} %param.7) | copy-start | bytes 49156
  1.1 14.1 %copy-start.2 = (f32[1,1,8,512]{3,2,1,0:T(8,128)S(1)}, f32[1,1,8,512]{3,2,1,0:T(8,128)}, u32[]{:S(2)}) copy-start(f32[1,1,8,512]{3,2,1,0:T(8,128)} %param.8) | copy-start | bytes 49156
  1.2 11.9 %collective-permute-start = (bf16[32,1024]{1,0:T(8,128)(2,1)S(1)}, bf16[32,1024]{1,0:T(8,128)(2,1)S(1)}, u32[]{:S(2)}, u32[]{:S(2)}) collective-permute-start(bf16[32,1024]{1,0:T(8,128)(2,1)S(1)} %get-tuple-element.36), channel_id=1, source_target_pairs={{0,24},{4,28},{8,16},{12,20},{16,8},{20,12},{24,0},{28,4},{1,25},{... | collective-permute-start | bytes 196616 | tf_op jit(solution)/shard_map/ppermute | solution.py:156
  6.3 7.6 %collective-permute-start.1 = (bf16[32,1024]{1,0:T(8,128)(2,1)S(1)}, bf16[32,1024]{1,0:T(8,128)(2,1)S(1)}, u32[]{:S(2)}, u32[]{:S(2)}) collective-permute-start(bf16[32,1024]{1,0:T(8,128)(2,1)S(1)} %get-tuple-element.35), channel_id=1, source_target_pairs={{0,20},{4,16},{8,28},{12,24},{16,4},{20,0},{24,12},{28,8},{1,21},{... | collective-permute-start | bytes 196616 | tf_op jit(solution)/shard_map/ppermute | solution.py:156
  6.7 8.6 %collective-permute-start.2 = (bf16[32,1024]{1,0:T(8,128)(2,1)S(1)}, bf16[32,1024]{1,0:T(8,128)(2,1)S(1)}, u32[]{:S(2)}, u32[]{:S(2)}) collective-permute-start(bf16[32,1024]{1,0:T(8,128)(2,1)S(1)} %get-tuple-element.34), channel_id=1, source_target_pairs={{0,12},{4,8},{8,4},{12,0},{16,28},{20,24},{24,20},{28,16},{1,13},{... | collective-permute-start | bytes 196616 | tf_op jit(solution)/shard_map/ppermute | solution.py:156
  7.8 9.5 %collective-permute-start.3 = (bf16[32,1024]{1,0:T(8,128)(2,1)S(1)}, bf16[32,1024]{1,0:T(8,128)(2,1)S(1)}, u32[]{:S(2)}, u32[]{:S(2)}) collective-permute-start(bf16[32,1024]{1,0:T(8,128)(2,1)S(1)} %get-tuple-element.33), channel_id=1, source_target_pairs={{0,28},{4,24},{8,20},{12,16},{16,12},{20,8},{24,4},{28,0},{1,29},{... | collective-permute-start | bytes 196616 | tf_op jit(solution)/shard_map/ppermute | solution.py:156
  12.5 4.8 %collective-permute-start.4 = (bf16[32,1024]{1,0:T(8,128)(2,1)S(1)}, bf16[32,1024]{1,0:T(8,128)(2,1)S(1)}, u32[]{:S(2)}, u32[]{:S(2)}) collective-permute-start(bf16[32,1024]{1,0:T(8,128)(2,1)S(1)} %get-tuple-element.32), channel_id=1, source_target_pairs={{0,8},{4,12},{8,0},{12,4},{16,24},{20,28},{24,16},{28,20},{1,9},{5... | collective-permute-start | bytes 196616 | tf_op jit(solution)/shard_map/ppermute | solution.py:156
  13.1 5.2 %collective-permute-start.5 = (bf16[32,1024]{1,0:T(8,128)(2,1)S(1)}, bf16[32,1024]{1,0:T(8,128)(2,1)S(1)}, u32[]{:S(2)}, u32[]{:S(2)}) collective-permute-start(bf16[32,1024]{1,0:T(8,128)(2,1)S(1)} %get-tuple-element.38), channel_id=1, source_target_pairs={{0,16},{4,20},{8,24},{12,28},{16,0},{20,4},{24,8},{28,12},{1,17},{... | collective-permute-start | bytes 196616 | tf_op jit(solution)/shard_map/ppermute | solution.py:156
  13.9 4.4 %collective-permute-start.6 = (bf16[32,1024]{1,0:T(8,128)(2,1)S(1)}, bf16[32,1024]{1,0:T(8,128)(2,1)S(1)}, u32[]{:S(2)}, u32[]{:S(2)}) collective-permute-start(bf16[32,1024]{1,0:T(8,128)(2,1)S(1)} %get-tuple-element.31), channel_id=1, source_target_pairs={{0,4},{4,0},{8,12},{12,8},{16,20},{20,16},{24,28},{28,24},{1,5},{5... | collective-permute-start | bytes 196616 | tf_op jit(solution)/shard_map/ppermute | solution.py:156
  27.0 8.9 %collective-permute-start.7 = (bf16[32,1024]{1,0:T(8,128)(2,1)S(1)}, bf16[32,1024]{1,0:T(8,128)(2,1)S(1)}, u32[]{:S(2)}, u32[]{:S(2)}) collective-permute-start(bf16[32,1024]{1,0:T(8,128)(2,1)S(1)} %get-tuple-element.24), channel_id=1, source_target_pairs={{0,24},{4,28},{8,16},{12,20},{16,8},{20,12},{24,0},{28,4},{1,25},{... | collective-permute-start | bytes 196616 | tf_op jit(solution)/shard_map/ppermute | solution.py:156
  30.6 7.0 %collective-permute-start.8 = (bf16[32,1024]{1,0:T(8,128)(2,1)S(1)}, bf16[32,1024]{1,0:T(8,128)(2,1)S(1)}, u32[]{:S(2)}, u32[]{:S(2)}) collective-permute-start(bf16[32,1024]{1,0:T(8,128)(2,1)S(1)} %get-tuple-element.25), channel_id=1, source_target_pairs={{0,20},{4,16},{8,28},{12,24},{16,4},{20,0},{24,12},{28,8},{1,21},{... | collective-permute-start | bytes 196616 | tf_op jit(solution)/shard_map/ppermute | solution.py:156
  30.6 8.0 %collective-permute-start.9 = (bf16[32,1024]{1,0:T(8,128)(2,1)S(1)}, bf16[32,1024]{1,0:T(8,128)(2,1)S(1)}, u32[]{:S(2)}, u32[]{:S(2)}) collective-permute-start(bf16[32,1024]{1,0:T(8,128)(2,1)S(1)} %get-tuple-element.26), channel_id=1, source_target_pairs={{0,12},{4,8},{8,4},{12,0},{16,28},{20,24},{24,20},{28,16},{1,13},{... | collective-permute-start | bytes 196616 | tf_op jit(solution)/shard_map/ppermute | solution.py:156
  32.4 7.4 %collective-permute-start.10 = (bf16[32,1024]{1,0:T(8,128)(2,1)S(1)}, bf16[32,1024]{1,0:T(8,128)(2,1)S(1)}, u32[]{:S(2)}, u32[]{:S(2)}) collective-permute-start(bf16[32,1024]{1,0:T(8,128)(2,1)S(1)} %get-tuple-element.27), channel_id=1, source_target_pairs={{0,28},{4,24},{8,20},{12,16},{16,12},{20,8},{24,4},{28,0},{1,29},{... | collective-permute-start | bytes 196616 | tf_op jit(solution)/shard_map/ppermute | solution.py:156
  35.9 4.6 %collective-permute-start.11 = (bf16[32,1024]{1,0:T(8,128)(2,1)S(1)}, bf16[32,1024]{1,0:T(8,128)(2,1)S(1)}, u32[]{:S(2)}, u32[]{:S(2)}) collective-permute-start(bf16[32,1024]{1,0:T(8,128)(2,1)S(1)} %get-tuple-element.28), channel_id=1, source_target_pairs={{0,8},{4,12},{8,0},{12,4},{16,24},{20,28},{24,16},{28,20},{1,9},{5... | collective-permute-start | bytes 196616 | tf_op jit(solution)/shard_map/ppermute | solution.py:156
  35.9 5.2 %collective-permute-start.12 = (bf16[32,1024]{1,0:T(8,128)(2,1)S(1)}, bf16[32,1024]{1,0:T(8,128)(2,1)S(1)}, u32[]{:S(2)}, u32[]{:S(2)}) collective-permute-start(bf16[32,1024]{1,0:T(8,128)(2,1)S(1)} %get-tuple-element.29), channel_id=1, source_target_pairs={{0,16},{4,20},{8,24},{12,28},{16,0},{20,4},{24,8},{28,12},{1,17},{... | collective-permute-start | bytes 196616 | tf_op jit(solution)/shard_map/ppermute | solution.py:156
  37.6 4.3 %collective-permute-start.13 = (bf16[32,1024]{1,0:T(8,128)(2,1)S(1)}, bf16[32,1024]{1,0:T(8,128)(2,1)S(1)}, u32[]{:S(2)}, u32[]{:S(2)}) collective-permute-start(bf16[32,1024]{1,0:T(8,128)(2,1)S(1)} %get-tuple-element.30), channel_id=1, source_target_pairs={{0,4},{4,0},{8,12},{12,8},{16,20},{20,16},{24,28},{28,24},{1,5},{5... | collective-permute-start | bytes 196616 | tf_op jit(solution)/shard_map/ppermute | solution.py:156
  41.2 0.8 %copy-start.4 = (bf16[32,8192]{1,0:T(8,128)(2,1)}, bf16[32,8192]{1,0:T(8,128)(2,1)S(1)}, u32[]{:S(2)}) copy-start(bf16[32,8192]{1,0:T(8,128)(2,1)S(1)} %constant_dynamic-update-slice_fusion.1) | copy-start | bytes 1572868

commit v3 on v2

--- a/solution.py
+++ b/solution.py
@@ -63,7 +63,7 @@
 
 def main_kernel(parts, early, index_ref, value_ref, weight_ref, picked_ref, total_ref, *refs):
     chunk_refs, out_refs = refs[:parts], refs[parts : 2 * parts]
-    anomaly_s, mean_s, pick_s = refs[2 * parts :]
+    anomaly_s, mean_s, late_s, pick_s = refs[2 * parts :]
     share, cells = chunk_refs[0].shape
     members = share * parts
     slots, nobs = index_ref.shape
@@ -78,31 +78,38 @@
     eye = (lax.broadcasted_iota(jnp.int32, square, 0) == lax.broadcasted_iota(jnp.int32, square, 1)).astype(F32)
     late = jnp.concatenate([ref[...] for ref in chunk_refs[early:]], axis=0)
     extra = lax.broadcasted_iota(jnp.int32, (PACKED_ROWS, nobs), 0) == 0
-    iterates, scales, rights = [], [], []
-    for block in range(slots):
-        line = slice(block, block + 1)
-        weight = weight_ref[line, :]
-        picked = pick_rows(late, index_ref[line, :], pick_s.at[block % 2], slots)
-        obs_mean = (total_ref[line, :] + jnp.sum(picked, axis=0, keepdims=True)) / members
-        innovation = weight * (value_ref[line, :] - obs_mean)
-        before = picked_ref[:, block * nobs : (block + 1) * nobs].astype(F32)
-        observed = jnp.concatenate([(before - obs_mean).astype(BF16), (picked - obs_mean).astype(BF16)], axis=0)
-        weighted = (observed.astype(F32) * weight).astype(BF16)
+    blocks = range(slots)
+    lines = [slice(block, block + 1) for block in blocks]
+    obs_means = []
+    for block in blocks:
+        picked = pick_rows(late, index_ref[lines[block], :], pick_s.at[block % 2], slots)
+        obs_means.append((total_ref[lines[block], :] + jnp.sum(picked, axis=0, keepdims=True)) / members)
+        late_s[:, block * nobs : (block + 1) * nobs] = picked.astype(BF16)
+    products = []
+    for block in blocks:
+        cols = slice(block * nobs, (block + 1) * nobs)
+        obs_mean, weight = obs_means[block], weight_ref[lines[block], :]
+        innovation = weight * (value_ref[lines[block], :] - obs_mean)
+        observed = jnp.concatenate(
+            [(ref[:, cols].astype(F32) - obs_mean).astype(BF16) for ref in (picked_ref, late_s)], axis=0
+        )
+        weighted = observed * weight.astype(BF16)
         left = jnp.concatenate([weighted, jnp.where(extra, innovation, 0.0).astype(BF16)], axis=0)
-        products = dot(left, observed, ((1,), (1,)))
-        rights.append(products[members : members + 1])
-        gram = products[:members] + (members - 1.0) * eye
+        products.append(dot(left, observed, ((1,), (1,))))
+    rights = [p[members : members + 1] for p in products]
+    iterates, scales = [], []
+    for block in blocks:
+        gram = products[block][:members] + (members - 1.0) * eye
         scale = jnp.sqrt(jnp.sum(jnp.sum(gram * gram, axis=0, keepdims=True), axis=1, keepdims=True))
         scales.append(scale)
         iterates.append((gram * (1.0 / scale)).astype(BF16))
     roots = newton_steps(iterates, eye)
-    for block in range(slots):
-        cols = slice(block * width, (block + 1) * width)
-        root, right, scale = roots[block], rights[block], scales[block]
-        inner = jnp.sum(root.astype(F32) * right, axis=1, keepdims=True)
-        moved = dot(root, anomaly_s[:, cols], ((0,), (0,)))
-        shift = jnp.sum(moved * inner, axis=0, keepdims=True) / scale + mean_s[block : block + 1, :]
-        result = (jnp.sqrt((members - 1.0) / scale) * moved + shift).astype(BF16)
+    moved = [dot(roots[k], anomaly_s[:, k * width : (k + 1) * width], ((0,), (0,))) for k in blocks]
+    inner = [jnp.sum(roots[k].astype(F32) * rights[k], axis=1, keepdims=True) for k in blocks]
+    for block in blocks:
+        cols, scale = slice(block * width, (block + 1) * width), scales[block]
+        shift = jnp.sum(moved[block] * inner[block], axis=0, keepdims=True) / scale + mean_s[lines[block], :]
+        result = (jnp.sqrt((members - 1.0) / scale) * moved[block] + shift).astype(BF16)
         for p, ref in enumerate(out_refs):
             ref[:, cols] = result[p * share : (p + 1) * share]
 
@@ -138,6 +145,7 @@
         scratch_shapes=[
             pltpu.VMEM((share * parts, cells), BF16),
             pltpu.VMEM((slots, cells // slots), F32),
+            pltpu.VMEM((share * (parts - early), slots * nobs), BF16),
             pltpu.VMEM((2, cells, nobs), BF16),
         ],
         compiler_params=pltpu.CompilerParams(vmem_limit_bytes=40 << 20),

time: 42.8 us -> 41.4 us (0.967)
  Pallas kernels: 10.8 us -> 9.45 us
    pallas_call x1, Pallas kernels: 8.76 us -> 7.43 us  [analyse(): pl.pallas_call(functools.partial(main_kernel, parts, early), out_shape=[j...]
where the time goes in v3:
time: 41.4 us; the launch traced here: 41.3 us
  starting transfers between devices  24.9 us (60%)
  Pallas kernels  9.45 us (23%)
  waiting for transfers between devices  4.3 us (10%)
  local copies, waits for them, and re-layouts  2.48 us (6%)
    ppermute x14, starting transfers between devices, exchange(): lax.ppermute(block, 'wide', [(i, i ^ step) for i in range(lax.axis_size('...  24.9 us
    pallas_call x1, Pallas kernels, analyse(): pl.pallas_call(functools.partial(main_kernel, parts, early), out_shape=[j...  7.43 us
    ppermute x14, waiting for transfers between devices, exchange(): lax.ppermute(block, 'wide', [(i, i ^ step) for i in range(lax.axis_size('...  4.3 us
    pallas_call x1, Pallas kernels, analyse(): pl.pallas_call(functools.partial(early_kernel, early), out_shape=[jax.Sha...  2.02 us
    dynamic_slice x1, local copies, waits for them, and re-layouts, per_device(): lax.dynamic_slice(fields, (0, (me ^ s) * cells), (share, cells))  1.12 us
  transfers between devices with their start and end apart: 14, of which 5 were waited for; matrix products, arithmetic and copies ran while one was open for 2% of the time, Pallas kernels for 5%

profile of v3, /device:TPU:0, one launch (start us, length us, event | category | flops | bytes accessed | tf_op | source)
XLA Modules:
  0.0 41.3 jit_solution(6413757591553285935)
XLA Ops:
  0.0 1.1 %constant_dynamic-slice_fusion = (bf16[32,1024]{1,0:T(8,128)(2,1)S(1)}, bf16[32,1024]{1,0:T(8,128)(2,1)S(1)}, bf16[32,1024]{1,0:T(8,128)(2,1)S(1)}, bf16[32,1024...) fusion(bf16[32,8192]{1,0:T(8,128)(2,1)} %param.5, ...), kind=kLoop, calls=%fused_computation.8 | loop fusion | bytes 1048608 | tf_op jit(solution)/shard_map/dynamic_slice | solution.py:180
  1.1 0.0 copy-start.1
  1.1 0.0 copy-start.2
  1.2 5.1 %collective-permute-start = (bf16[32,1024]{1,0:T(8,128)(2,1)S(1)}, bf16[32,1024]{1,0:T(8,128)(2,1)S(1)}, u32[]{:S(2)}, u32[]{:S(2)}) collective-permute-start(bf16[32,1024]{1,0:T(8,128)(2,1)S(1)} %get-tuple-element.36), channel_id=1, source_target_pairs={{0,24},{4,28},{8,16},{12,20},{16,8},{20,12},{24,0},{28,4},{1,25},{... | collective-permute-start | bytes 196616 | tf_op jit(solution)/shard_map/ppermute | solution.py:164
  6.3 0.4 collective-permute-start.1
  6.7 1.2 %collective-permute-start.2 = (bf16[32,1024]{1,0:T(8,128)(2,1)S(1)}, bf16[32,1024]{1,0:T(8,128)(2,1)S(1)}, u32[]{:S(2)}, u32[]{:S(2)}) collective-permute-start(bf16[32,1024]{1,0:T(8,128)(2,1)S(1)} %get-tuple-element.34), channel_id=1, source_target_pairs={{0,12},{4,8},{8,4},{12,0},{16,28},{20,24},{24,20},{28,16},{1,13},{... | collective-permute-start | bytes 196616 | tf_op jit(solution)/shard_map/ppermute | solution.py:164
  7.8 4.7 %collective-permute-start.3 = (bf16[32,1024]{1,0:T(8,128)(2,1)S(1)}, bf16[32,1024]{1,0:T(8,128)(2,1)S(1)}, u32[]{:S(2)}, u32[]{:S(2)}) collective-permute-start(bf16[32,1024]{1,0:T(8,128)(2,1)S(1)} %get-tuple-element.33), channel_id=1, source_target_pairs={{0,28},{4,24},{8,20},{12,16},{16,12},{20,8},{24,4},{28,0},{1,29},{... | collective-permute-start | bytes 196616 | tf_op jit(solution)/shard_map/ppermute | solution.py:164
  12.5 0.0 collective-permute-start.4
  12.5 0.6 %constant_dynamic-slice_fusion.8 = s32[1,1]{0,1:T(1,128)} fusion(s32[4,1]{0,1:T(1,128)S(1)} %copy-done, s32[]{:T(128)S(6)} %select_n.35), kind=kLoop, calls=%fused_computation.16 | loop fusion | bytes 12 | tf_op jit(solution)/shard_map/dynamic_slice | solution.py:171
  13.1 0.0 collective-permute-done.refs_1_
  13.1 0.8 %collective-permute-start.5 = (bf16[32,1024]{1,0:T(8,128)(2,1)S(1)}, bf16[32,1024]{1,0:T(8,128)(2,1)S(1)}, u32[]{:S(2)}, u32[]{:S(2)}) collective-permute-start(bf16[32,1024]{1,0:T(8,128)(2,1)S(1)} %get-tuple-element.38), channel_id=1, source_target_pairs={{0,16},{4,20},{8,24},{12,28},{16,0},{20,4},{24,8},{28,12},{1,17},{... | collective-permute-start | bytes 196616 | tf_op jit(solution)/shard_map/ppermute | solution.py:164
  13.9 1.4 %collective-permute-start.6 = (bf16[32,1024]{1,0:T(8,128)(2,1)S(1)}, bf16[32,1024]{1,0:T(8,128)(2,1)S(1)}, u32[]{:S(2)}, u32[]{:S(2)}) collective-permute-start(bf16[32,1024]{1,0:T(8,128)(2,1)S(1)} %get-tuple-element.31), channel_id=1, source_target_pairs={{0,4},{4,0},{8,12},{12,8},{16,20},{20,16},{24,28},{28,24},{1,5},{5... | collective-permute-start | bytes 196616 | tf_op jit(solution)/shard_map/ppermute | solution.py:164
  15.3 2.0 %shard_map.55 = (bf16[128,4096]{1,0:T(8,128)(2,1)S(1)}, f32[8,512]{1,0:T(8,128)S(1)}, s32[8,512]{1,0:T(8,128)S(1)}, f32[8,512]{1,0:T(8,128)S(1)}, f32[8,512]{1,0:T(8,128)S(1)}) custom-call(s32[1]{0:T(128)} %bitcast.count_ref, s32[8,512]{1,0:T(8,128)S(1)} %bitcast.4, f32[8,512]{1,0:T(8,128)S(1)} %bitcast.5, bf16[8,512]{1,0:T(8,128)(2,1)S(1)} %bitcast.6, ...), custom_call_target="tpu_custom_call" | custom-call | flops 1073741824 | bytes 1048576 | tf_op jit(solution)/shard_map/pallas_call | solution.py:123
  17.3 0.0 collective-permute-done.3.refs_4_
  17.3 1.0 %collective-permute-done.5.refs_6_ = bf16[32,1024]{1,0:T(8,128)(2,1)S(1)} collective-permute-done((bf16[32,1024]{1,0:T(8,128)(2,1)S(1)}, bf16[32,1024]{1,0:T(8,128)(2,1)S(1)}, u32[]{:S(2)}, u32[]{:S(2)}) %collective-permute-start.5) | collective-permute-done | bytes 65568 | tf_op jit(solution)/shard_map/ppermute | solution.py:164
  18.3 7.4 %shard_map.56 = (bf16[32,1024]{1,0:T(8,128)(2,1)S(1)}, bf16[32,1024]{1,0:T(8,128)(2,1)S(1)}, bf16[32,1024]{1,0:T(8,128)(2,1)S(1)}, bf16[32,1024]{1,0:T(8,128)(2,...) custom-call(s32[8,512]{1,0:T(8,128)S(1)} %get-tuple-element.18.index, ...), custom_call_target="tpu_custom_call" | custom-call | tf_op jit(solution)/shard_map/pallas_call | solution.py:140
  25.7 3.5 %collective-permute-start.7 = (bf16[32,1024]{1,0:T(8,128)(2,1)S(1)}, bf16[32,1024]{1,0:T(8,128)(2,1)S(1)}, u32[]{:S(2)}, u32[]{:S(2)}) collective-permute-start(bf16[32,1024]{1,0:T(8,128)(2,1)S(1)} %get-tuple-element.24), channel_id=1, source_target_pairs={{0,24},{4,28},{8,16},{12,20},{16,8},{20,12},{24,0},{28,4},{1,25},{... | collective-permute-start | bytes 196616 | tf_op jit(solution)/shard_map/ppermute | solution.py:164
  29.3 1.8 %collective-permute-start.9 = (bf16[32,1024]{1,0:T(8,128)(2,1)S(1)}, bf16[32,1024]{1,0:T(8,128)(2,1)S(1)}, u32[]{:S(2)}, u32[]{:S(2)}) collective-permute-start(bf16[32,1024]{1,0:T(8,128)(2,1)S(1)} %get-tuple-element.26), channel_id=1, source_target_pairs={{0,12},{4,8},{8,4},{12,0},{16,28},{20,24},{24,20},{28,16},{1,13},{... | collective-permute-start | bytes 196616 | tf_op jit(solution)/shard_map/ppermute | solution.py:164
  31.1 3.5 %collective-permute-start.10 = (bf16[32,1024]{1,0:T(8,128)(2,1)S(1)}, bf16[32,1024]{1,0:T(8,128)(2,1)S(1)}, u32[]{:S(2)}, u32[]{:S(2)}) collective-permute-start(bf16[32,1024]{1,0:T(8,128)(2,1)S(1)} %get-tuple-element.27), channel_id=1, source_target_pairs={{0,28},{4,24},{8,20},{12,16},{16,12},{20,8},{24,4},{28,0},{1,29},{... | collective-permute-start | bytes 196616 | tf_op jit(solution)/shard_map/ppermute | solution.py:164
  34.5 0.0 collective-permute-start.11
  34.6 0.0 collective-permute-done.7
  34.6 1.7 %collective-permute-start.12 = (bf16[32,1024]{1,0:T(8,128)(2,1)S(1)}, bf16[32,1024]{1,0:T(8,128)(2,1)S(1)}, u32[]{:S(2)}, u32[]{:S(2)}) collective-permute-start(bf16[32,1024]{1,0:T(8,128)(2,1)S(1)} %get-tuple-element.29), channel_id=1, source_target_pairs={{0,16},{4,20},{8,24},{12,28},{16,0},{20,4},{24,8},{28,12},{1,17},{... | collective-permute-start | bytes 196616 | tf_op jit(solution)/shard_map/ppermute | solution.py:164
  36.3 0.0 collective-permute-done.8
  36.3 0.9 %collective-permute-start.13 = (bf16[32,1024]{1,0:T(8,128)(2,1)S(1)}, bf16[32,1024]{1,0:T(8,128)(2,1)S(1)}, u32[]{:S(2)}, u32[]{:S(2)}) collective-permute-start(bf16[32,1024]{1,0:T(8,128)(2,1)S(1)} %get-tuple-element.30), channel_id=1, source_target_pairs={{0,4},{4,0},{8,12},{12,8},{16,20},{20,16},{24,28},{28,24},{1,5},{5... | collective-permute-start | bytes 196616 | tf_op jit(solution)/shard_map/ppermute | solution.py:164
  37.2 0.0 collective-permute-done.9
  37.2 1.2 %collective-permute-done.10 = bf16[32,1024]{1,0:T(8,128)(2,1)S(1)} collective-permute-done((bf16[32,1024]{1,0:T(8,128)(2,1)S(1)}, bf16[32,1024]{1,0:T(8,128)(2,1)S(1)}, u32[]{:S(2)}, u32[]{:S(2)}) %collective-permute-start.10) | collective-permute-done | bytes 65568 | tf_op jit(solution)/shard_map/ppermute | solution.py:164
  38.5 0.6 %collective-permute-done.11 = bf16[32,1024]{1,0:T(8,128)(2,1)S(1)} collective-permute-done((bf16[32,1024]{1,0:T(8,128)(2,1)S(1)}, bf16[32,1024]{1,0:T(8,128)(2,1)S(1)}, u32[]{:S(2)}, u32[]{:S(2)}) %collective-permute-start.11) | collective-permute-done | bytes 65568 | tf_op jit(solution)/shard_map/ppermute | solution.py:164
  39.1 0.7 %collective-permute-done.12 = bf16[32,1024]{1,0:T(8,128)(2,1)S(1)} collective-permute-done((bf16[32,1024]{1,0:T(8,128)(2,1)S(1)}, bf16[32,1024]{1,0:T(8,128)(2,1)S(1)}, u32[]{:S(2)}, u32[]{:S(2)}) %collective-permute-start.12) | collective-permute-done | bytes 65568 | tf_op jit(solution)/shard_map/ppermute | solution.py:164
  39.8 0.0 copy-start.4
  39.8 0.8 %collective-permute-done.13 = bf16[32,1024]{1,0:T(8,128)(2,1)S(1)} collective-permute-done((bf16[32,1024]{1,0:T(8,128)(2,1)S(1)}, bf16[32,1024]{1,0:T(8,128)(2,1)S(1)}, u32[]{:S(2)}, u32[]{:S(2)}) %collective-permute-start.13) | collective-permute-done | bytes 65568 | tf_op jit(solution)/shard_map/ppermute | solution.py:164
  40.6 0.0 copy-done.4
  40.6 0.6 %constant_dynamic-update-slice_fusion = bf16[32,8192]{1,0:T(8,128)(2,1)} fusion(bf16[32,8192]{1,0:T(8,128)(2,1)} %copy-done.4, bf16[32,1024]{1,0:T(8,128)(2,1)S(1)} %collective-permute-done.13, s32[]{:T(128)S(6)} %select_n.43), kind=kLoop, calls=%fused_computation | loop fusion | bytes 131076 | tf_op jit(solution)/shard_map/dynamic_update_slice | solution.py:186
  (19 shorter events, 0.1 us)
Async XLA Ops:
  0.0 12.5 %copy-start = (s32[4,1]{0,1:T(1,128)S(1)}, s32[4,1]{0,1:T(1,128)}, u32[]{:S(2)}) copy-start(s32[4,1]{0,1:T(1,128)} %param.6) | copy-start | bytes 52
  0.0 15.3 %copy-start.3 = (bf16[1,1,8,512]{3,2,1,0:T(8,128)(2,1)S(1)}, bf16[1,1,8,512]{3,2,1,0:T(8,128)(2,1)}, u32[]{:S(2)}) copy-start(bf16[1,1,8,512]{3,2,1,0:T(8,128)(2,1)} %param.9) | copy-start | bytes 24580
  1.1 14.1 %copy-start.1 = (s32[1,1,8,512]{3,2,1,0:T(8,128)S(1)}, s32[1,1,8,512]{3,2,1,0:T(8,128)}, u32[]{:S(2)}) copy-start(s32[1,1,8,512]{3,2,1,0:T(8,128)} %param.7) | copy-start | bytes 49156
  1.1 14.1 %copy-start.2 = (f32[1,1,8,512]{3,2,1,0:T(8,128)S(1)}, f32[1,1,8,512]{3,2,1,0:T(8,128)}, u32[]{:S(2)}) copy-start(f32[1,1,8,512]{3,2,1,0:T(8,128)} %param.8) | copy-start | bytes 49156
  1.2 11.9 %collective-permute-start = (bf16[32,1024]{1,0:T(8,128)(2,1)S(1)}, bf16[32,1024]{1,0:T(8,128)(2,1)S(1)}, u32[]{:S(2)}, u32[]{:S(2)}) collective-permute-start(bf16[32,1024]{1,0:T(8,128)(2,1)S(1)} %get-tuple-element.36), channel_id=1, source_target_pairs={{0,24},{4,28},{8,16},{12,20},{16,8},{20,12},{24,0},{28,4},{1,25},{... | collective-permute-start | bytes 196616 | tf_op jit(solution)/shard_map/ppermute | solution.py:164
  6.3 7.6 %collective-permute-start.1 = (bf16[32,1024]{1,0:T(8,128)(2,1)S(1)}, bf16[32,1024]{1,0:T(8,128)(2,1)S(1)}, u32[]{:S(2)}, u32[]{:S(2)}) collective-permute-start(bf16[32,1024]{1,0:T(8,128)(2,1)S(1)} %get-tuple-element.35), channel_id=1, source_target_pairs={{0,20},{4,16},{8,28},{12,24},{16,4},{20,0},{24,12},{28,8},{1,21},{... | collective-permute-start | bytes 196616 | tf_op jit(solution)/shard_map/ppermute | solution.py:164
  6.7 8.6 %collective-permute-start.2 = (bf16[32,1024]{1,0:T(8,128)(2,1)S(1)}, bf16[32,1024]{1,0:T(8,128)(2,1)S(1)}, u32[]{:S(2)}, u32[]{:S(2)}) collective-permute-start(bf16[32,1024]{1,0:T(8,128)(2,1)S(1)} %get-tuple-element.34), channel_id=1, source_target_pairs={{0,12},{4,8},{8,4},{12,0},{16,28},{20,24},{24,20},{28,16},{1,13},{... | collective-permute-start | bytes 196616 | tf_op jit(solution)/shard_map/ppermute | solution.py:164
  7.8 9.5 %collective-permute-start.3 = (bf16[32,1024]{1,0:T(8,128)(2,1)S(1)}, bf16[32,1024]{1,0:T(8,128)(2,1)S(1)}, u32[]{:S(2)}, u32[]{:S(2)}) collective-permute-start(bf16[32,1024]{1,0:T(8,128)(2,1)S(1)} %get-tuple-element.33), channel_id=1, source_target_pairs={{0,28},{4,24},{8,20},{12,16},{16,12},{20,8},{24,4},{28,0},{1,29},{... | collective-permute-start | bytes 196616 | tf_op jit(solution)/shard_map/ppermute | solution.py:164
  12.5 4.8 %collective-permute-start.4 = (bf16[32,1024]{1,0:T(8,128)(2,1)S(1)}, bf16[32,1024]{1,0:T(8,128)(2,1)S(1)}, u32[]{:S(2)}, u32[]{:S(2)}) collective-permute-start(bf16[32,1024]{1,0:T(8,128)(2,1)S(1)} %get-tuple-element.32), channel_id=1, source_target_pairs={{0,8},{4,12},{8,0},{12,4},{16,24},{20,28},{24,16},{28,20},{1,9},{5... | collective-permute-start | bytes 196616 | tf_op jit(solution)/shard_map/ppermute | solution.py:164
  13.1 5.2 %collective-permute-start.5 = (bf16[32,1024]{1,0:T(8,128)(2,1)S(1)}, bf16[32,1024]{1,0:T(8,128)(2,1)S(1)}, u32[]{:S(2)}, u32[]{:S(2)}) collective-permute-start(bf16[32,1024]{1,0:T(8,128)(2,1)S(1)} %get-tuple-element.38), channel_id=1, source_target_pairs={{0,16},{4,20},{8,24},{12,28},{16,0},{20,4},{24,8},{28,12},{1,17},{... | collective-permute-start | bytes 196616 | tf_op jit(solution)/shard_map/ppermute | solution.py:164
  13.9 4.4 %collective-permute-start.6 = (bf16[32,1024]{1,0:T(8,128)(2,1)S(1)}, bf16[32,1024]{1,0:T(8,128)(2,1)S(1)}, u32[]{:S(2)}, u32[]{:S(2)}) collective-permute-start(bf16[32,1024]{1,0:T(8,128)(2,1)S(1)} %get-tuple-element.31), channel_id=1, source_target_pairs={{0,4},{4,0},{8,12},{12,8},{16,20},{20,16},{24,28},{28,24},{1,5},{5... | collective-permute-start | bytes 196616 | tf_op jit(solution)/shard_map/ppermute | solution.py:164
  25.7 8.9 %collective-permute-start.7 = (bf16[32,1024]{1,0:T(8,128)(2,1)S(1)}, bf16[32,1024]{1,0:T(8,128)(2,1)S(1)}, u32[]{:S(2)}, u32[]{:S(2)}) collective-permute-start(bf16[32,1024]{1,0:T(8,128)(2,1)S(1)} %get-tuple-element.24), channel_id=1, source_target_pairs={{0,24},{4,28},{8,16},{12,20},{16,8},{20,12},{24,0},{28,4},{1,25},{... | collective-permute-start | bytes 196616 | tf_op jit(solution)/shard_map/ppermute | solution.py:164
  29.3 7.0 %collective-permute-start.8 = (bf16[32,1024]{1,0:T(8,128)(2,1)S(1)}, bf16[32,1024]{1,0:T(8,128)(2,1)S(1)}, u32[]{:S(2)}, u32[]{:S(2)}) collective-permute-start(bf16[32,1024]{1,0:T(8,128)(2,1)S(1)} %get-tuple-element.25), channel_id=1, source_target_pairs={{0,20},{4,16},{8,28},{12,24},{16,4},{20,0},{24,12},{28,8},{1,21},{... | collective-permute-start | bytes 196616 | tf_op jit(solution)/shard_map/ppermute | solution.py:164
  29.3 8.0 %collective-permute-start.9 = (bf16[32,1024]{1,0:T(8,128)(2,1)S(1)}, bf16[32,1024]{1,0:T(8,128)(2,1)S(1)}, u32[]{:S(2)}, u32[]{:S(2)}) collective-permute-start(bf16[32,1024]{1,0:T(8,128)(2,1)S(1)} %get-tuple-element.26), channel_id=1, source_target_pairs={{0,12},{4,8},{8,4},{12,0},{16,28},{20,24},{24,20},{28,16},{1,13},{... | collective-permute-start | bytes 196616 | tf_op jit(solution)/shard_map/ppermute | solution.py:164
  31.1 7.4 %collective-permute-start.10 = (bf16[32,1024]{1,0:T(8,128)(2,1)S(1)}, bf16[32,1024]{1,0:T(8,128)(2,1)S(1)}, u32[]{:S(2)}, u32[]{:S(2)}) collective-permute-start(bf16[32,1024]{1,0:T(8,128)(2,1)S(1)} %get-tuple-element.27), channel_id=1, source_target_pairs={{0,28},{4,24},{8,20},{12,16},{16,12},{20,8},{24,4},{28,0},{1,29},{... | collective-permute-start | bytes 196616 | tf_op jit(solution)/shard_map/ppermute | solution.py:164
  34.5 4.6 %collective-permute-start.11 = (bf16[32,1024]{1,0:T(8,128)(2,1)S(1)}, bf16[32,1024]{1,0:T(8,128)(2,1)S(1)}, u32[]{:S(2)}, u32[]{:S(2)}) collective-permute-start(bf16[32,1024]{1,0:T(8,128)(2,1)S(1)} %get-tuple-element.28), channel_id=1, source_target_pairs={{0,8},{4,12},{8,0},{12,4},{16,24},{20,28},{24,16},{28,20},{1,9},{5... | collective-permute-start | bytes 196616 | tf_op jit(solution)/shard_map/ppermute | solution.py:164
  34.6 5.2 %collective-permute-start.12 = (bf16[32,1024]{1,0:T(8,128)(2,1)S(1)}, bf16[32,1024]{1,0:T(8,128)(2,1)S(1)}, u32[]{:S(2)}, u32[]{:S(2)}) collective-permute-start(bf16[32,1024]{1,0:T(8,128)(2,1)S(1)} %get-tuple-element.29), channel_id=1, source_target_pairs={{0,16},{4,20},{8,24},{12,28},{16,0},{20,4},{24,8},{28,12},{1,17},{... | collective-permute-start | bytes 196616 | tf_op jit(solution)/shard_map/ppermute | solution.py:164
  36.3 4.3 %collective-permute-start.13 = (bf16[32,1024]{1,0:T(8,128)(2,1)S(1)}, bf16[32,1024]{1,0:T(8,128)(2,1)S(1)}, u32[]{:S(2)}, u32[]{:S(2)}) collective-permute-start(bf16[32,1024]{1,0:T(8,128)(2,1)S(1)} %get-tuple-element.30), channel_id=1, source_target_pairs={{0,4},{4,0},{8,12},{12,8},{16,20},{20,16},{24,28},{28,24},{1,5},{5... | collective-permute-start | bytes 196616 | tf_op jit(solution)/shard_map/ppermute | solution.py:164
  39.8 0.8 %copy-start.4 = (bf16[32,8192]{1,0:T(8,128)(2,1)}, bf16[32,8192]{1,0:T(8,128)(2,1)S(1)}, u32[]{:S(2)}) copy-start(bf16[32,8192]{1,0:T(8,128)(2,1)S(1)} %constant_dynamic-update-slice_fusion.1) | copy-start | bytes 1572868

commit v4 on v3

--- a/solution.py
+++ b/solution.py
@@ -9,7 +9,7 @@
 
 
 NS_ITERS = 6
-PARTNERS = (6, 5, 3, 7, 2, 4, 1)
+PARTNERS = {"in": (6, 5, 3, 7, 2, 4, 1), "out": (7, 5, 6, 3, 2, 4, 1)}
 PACKED_ROWS = 16
 F32 = jnp.float32
 BF16 = jnp.bfloat16
@@ -34,7 +34,7 @@
 
 def early_kernel(parts, count_ref, index_ref, value_ref, weight_ref, *refs):
     chunk_refs = refs[:parts]
-    picked_ref, total_ref, index_out, value_out, weight_out, weight_s, pick_s = refs[parts:]
+    picked_ref, index_out, value_out, weight_out, weight_s, pick_s = refs[parts:]
     slots, nobs = index_ref.shape
     count = count_ref[0]
     weight_s[...] = weight_ref[...].astype(F32)
@@ -46,22 +46,23 @@
         value_out[block : block + 1, :] = value_ref[pl.ds(slot, 1), :]
         weight_out[block : block + 1, :] = weight_s[pl.ds(slot, 1), :]
         picked = pick_rows(rows, index, pick_s.at[block % 2], slots)
-        total_ref[block : block + 1, :] = jnp.sum(picked, axis=0, keepdims=True)
         picked_ref[:, block * nobs : (block + 1) * nobs] = picked.astype(BF16)
 
 
 def newton_steps(iterates, eye):
     roots = [None] * len(iterates)
     for step in range(NS_ITERS):
-        products = iterates if step == 0 else [dot(r, y) for r, y in zip(roots, iterates)]
-        factors = [(1.5 * eye - 0.5 * p.astype(F32)).astype(BF16) for p in products]
+        if step == 0:
+            factors = [(1.5 * eye).astype(BF16) - BF16(0.5) * y for y in iterates]
+        else:
+            factors = [(1.5 * eye - 0.5 * dot(r, y)).astype(BF16) for r, y in zip(roots, iterates)]
         if step < NS_ITERS - 1:
             iterates = [dot(y, f).astype(BF16) for y, f in zip(iterates, factors)]
         roots = factors if step == 0 else [dot(f, r).astype(BF16) for f, r in zip(factors, roots)]
     return roots
 
 
-def main_kernel(parts, early, index_ref, value_ref, weight_ref, picked_ref, total_ref, *refs):
+def main_kernel(parts, early, index_ref, value_ref, weight_ref, picked_ref, *refs):
     chunk_refs, out_refs = refs[:parts], refs[parts : 2 * parts]
     anomaly_s, mean_s, late_s, pick_s = refs[2 * parts :]
     share, cells = chunk_refs[0].shape
@@ -76,23 +77,28 @@
         mean_s[j : j + 1, :] = mean[:, j * width : (j + 1) * width]
     square = (members, members)
     eye = (lax.broadcasted_iota(jnp.int32, square, 0) == lax.broadcasted_iota(jnp.int32, square, 1)).astype(F32)
-    late = jnp.concatenate([ref[...] for ref in chunk_refs[early:]], axis=0)
+    high = mean.astype(BF16).astype(F32)
+    middle = (mean - high).astype(BF16).astype(F32)
+    row = lax.broadcasted_iota(jnp.int32, (PACKED_ROWS, cells), 0)
+    mean_rows = jnp.where(row == 0, high, jnp.where(row == 1, middle, jnp.where(row == 2, mean - high - middle, 0.0)))
+    anomaly_s[members:, :] = mean_rows.astype(BF16)
+    late = anomaly_s[share * early :, :]
+    late_rows = members - share * early
     extra = lax.broadcasted_iota(jnp.int32, (PACKED_ROWS, nobs), 0) == 0
     blocks = range(slots)
     lines = [slice(block, block + 1) for block in blocks]
     obs_means = []
     for block in blocks:
         picked = pick_rows(late, index_ref[lines[block], :], pick_s.at[block % 2], slots)
-        obs_means.append((total_ref[lines[block], :] + jnp.sum(picked, axis=0, keepdims=True)) / members)
-        late_s[:, block * nobs : (block + 1) * nobs] = picked.astype(BF16)
+        obs_means.append(sum(picked[late_rows + k : late_rows + k + 1] for k in range(3)))
+        late_s[:, block * nobs : (block + 1) * nobs] = picked[:late_rows].astype(BF16)
     products = []
     for block in blocks:
         cols = slice(block * nobs, (block + 1) * nobs)
         obs_mean, weight = obs_means[block], weight_ref[lines[block], :]
         innovation = weight * (value_ref[lines[block], :] - obs_mean)
-        observed = jnp.concatenate(
-            [(ref[:, cols].astype(F32) - obs_mean).astype(BF16) for ref in (picked_ref, late_s)], axis=0
-        )
+        before = (picked_ref[:, cols].astype(F32) - obs_mean).astype(BF16)
+        observed = jnp.concatenate([before, late_s[:, cols]], axis=0)
         weighted = observed * weight.astype(BF16)
         left = jnp.concatenate([weighted, jnp.where(extra, innovation, 0.0).astype(BF16)], axis=0)
         products.append(dot(left, observed, ((1,), (1,))))
@@ -104,7 +110,7 @@
         scales.append(scale)
         iterates.append((gram * (1.0 / scale)).astype(BF16))
     roots = newton_steps(iterates, eye)
-    moved = [dot(roots[k], anomaly_s[:, k * width : (k + 1) * width], ((0,), (0,))) for k in blocks]
+    moved = [dot(roots[k], anomaly_s[:members, k * width : (k + 1) * width], ((0,), (0,))) for k in blocks]
     inner = [jnp.sum(roots[k].astype(F32) * rights[k], axis=1, keepdims=True) for k in blocks]
     for block in blocks:
         cols, scale = slice(block * width, (block + 1) * width), scales[block]
@@ -120,17 +126,16 @@
     slots, nobs = index.shape
     line = jax.ShapeDtypeStruct((slots, nobs), F32)
     rows = share * early
-    picked, total, index, value, weight = pl.pallas_call(
+    picked, index, value, weight = pl.pallas_call(
         functools.partial(early_kernel, early),
         out_shape=[
             jax.ShapeDtypeStruct((rows, slots * nobs), BF16),
-            line,
             jax.ShapeDtypeStruct((slots, nobs), jnp.int32),
             line,
             line,
         ],
         in_specs=[SMEM] + [VMEM] * (3 + early),
-        out_specs=[VMEM] * 5,
+        out_specs=[VMEM] * 4,
         scratch_shapes=[pltpu.VMEM((slots, nobs), F32), pltpu.VMEM((2, cells, nobs), BF16)],
         cost_estimate=pl.CostEstimate(
             flops=2 * rows * cells * slots * nobs, bytes_accessed=rows * slots * nobs * 2, transcendentals=0
@@ -140,20 +145,21 @@
     return pl.pallas_call(
         functools.partial(main_kernel, parts, early),
         out_shape=[jax.ShapeDtypeStruct((share, cells), BF16)] * parts,
-        in_specs=[VMEM] * (5 + parts),
+        in_specs=[VMEM] * (4 + parts),
         out_specs=[VMEM] * parts,
         scratch_shapes=[
-            pltpu.VMEM((share * parts, cells), BF16),
+            pltpu.VMEM((share * parts + PACKED_ROWS, cells), BF16),
             pltpu.VMEM((slots, cells // slots), F32),
             pltpu.VMEM((share * (parts - early), slots * nobs), BF16),
             pltpu.VMEM((2, cells, nobs), BF16),
         ],
         compiler_params=pltpu.CompilerParams(vmem_limit_bytes=40 << 20),
-    )(index, value, weight, picked, total, *chunks)
-
-
-def partner_order(parts):
-    return tuple(s for s in PARTNERS if s < parts) + tuple(range(len(PARTNERS) + 1, parts))
+    )(index, value, weight, picked, *chunks)
+
+
+def partner_order(way, parts):
+    known = PARTNERS[way]
+    return tuple(s for s in known if s < parts) + tuple(range(len(known) + 1, parts))
 
 
 def by_permutes(parts, share):
@@ -175,14 +181,15 @@
         half = whole.shape[0] // 2
         result = jnp.concatenate(analyse([whole[:half], whole[half:]], 1, *tile), axis=0)
         return lax.all_to_all(result, "wide", split_axis=0, concat_axis=1, tiled=True)
-    order = partner_order(parts)
+    order = partner_order("in", parts)
     steps = (0,) + order
     blocks = [lax.dynamic_slice(fields, (0, (me ^ s) * cells), (share, cells)) for s in steps]
     chunks = [blocks[0]] + [exchange(b, s) for b, s in zip(blocks[1:], order)]
-    results = analyse(chunks, parts // 2, *tile)
-    returned = [results[0]] + [exchange(b, s) for b, s in zip(results[1:], order)]
+    results = dict(zip(steps, analyse(chunks, parts // 2, *tile)))
+    order = partner_order("out", parts)
+    returned = [results[0]] + [exchange(results[s], s) for s in order]
     analysis = jnp.zeros_like(fields)
-    for s, block in zip(steps, returned):
+    for s, block in zip((0,) + order, returned):
         analysis = lax.dynamic_update_slice(analysis, block, (0, (me ^ s) * cells))
     return analysis
 

time: 41.4 us -> 42.9 us (1.036)
  waiting for transfers between devices: 4.3 us -> 6.09 us
    ppermute x14, waiting for transfers between devices: 4.3 us -> 6.09 us  [exchange(): lax.ppermute(block, 'wide', [(i, i ^ step) for i in range(lax.axis_size('...]
  transfers between devices with their start and end apart: 14 -> 14, of which waited for: 5 -> 4; matrix products, arithmetic and copies ran while one was open for 2% -> 2% of each run, Pallas kernels for 5% -> 5%
where the time goes in v4:
time: 42.9 us; the launch traced here: 42.7 us
  starting transfers between devices  24.7 us (58%)
  Pallas kernels  9.31 us (22%)
  waiting for transfers between devices  6.09 us (14%)
  local copies, waits for them, and re-layouts  2.48 us (6%)
    ppermute x14, starting transfers between devices, exchange(): lax.ppermute(block, 'wide', [(i, i ^ step) for i in range(lax.axis_size('...  24.7 us
    pallas_call x1, Pallas kernels, analyse(): pl.pallas_call(functools.partial(main_kernel, parts, early), out_shape=[j...  7.32 us
    ppermute x14, waiting for transfers between devices, exchange(): lax.ppermute(block, 'wide', [(i, i ^ step) for i in range(lax.axis_size('...  6.09 us
    pallas_call x1, Pallas kernels, analyse(): pl.pallas_call(functools.partial(early_kernel, early), out_shape=[jax.Sha...  2 us
    dynamic_slice x1, local copies, waits for them, and re-layouts, per_device(): lax.dynamic_slice(fields, (0, (me ^ s) * cells), (share, cells))  1.12 us
  transfers between devices with their start and end apart: 14, of which 4 were waited for; matrix products, arithmetic and copies ran while one was open for 2% of the time, Pallas kernels for 5%

profile of v4, /device:TPU:0, one launch (start us, length us, event | category | flops | bytes accessed | tf_op | source)
XLA Modules:
  0.0 42.7 jit_solution(11543698814152514357)
XLA Ops:
  0.0 1.1 %constant_dynamic-slice_fusion = (bf16[32,1024]{1,0:T(8,128)(2,1)S(1)}, bf16[32,1024]{1,0:T(8,128)(2,1)S(1)}, bf16[32,1024]{1,0:T(8,128)(2,1)S(1)}, bf16[32,1024...) fusion(bf16[32,8192]{1,0:T(8,128)(2,1)} %param.5, ...), kind=kLoop, calls=%fused_computation.8 | loop fusion | bytes 1048608 | tf_op jit(solution)/shard_map/dynamic_slice | solution.py:186
  1.1 0.0 copy-start.1
  1.1 0.0 copy-start.2
  1.2 5.1 %collective-permute-start = (bf16[32,1024]{1,0:T(8,128)(2,1)S(1)}, bf16[32,1024]{1,0:T(8,128)(2,1)S(1)}, u32[]{:S(2)}, u32[]{:S(2)}) collective-permute-start(bf16[32,1024]{1,0:T(8,128)(2,1)S(1)} %get-tuple-element.34), channel_id=1, source_target_pairs={{0,24},{4,28},{8,16},{12,20},{16,8},{20,12},{24,0},{28,4},{1,25},{... | collective-permute-start | bytes 196616 | tf_op jit(solution)/shard_map/ppermute | solution.py:170
  6.3 0.4 collective-permute-start.1
  6.7 1.2 %collective-permute-start.2 = (bf16[32,1024]{1,0:T(8,128)(2,1)S(1)}, bf16[32,1024]{1,0:T(8,128)(2,1)S(1)}, u32[]{:S(2)}, u32[]{:S(2)}) collective-permute-start(bf16[32,1024]{1,0:T(8,128)(2,1)S(1)} %get-tuple-element.32), channel_id=1, source_target_pairs={{0,12},{4,8},{8,4},{12,0},{16,28},{20,24},{24,20},{28,16},{1,13},{... | collective-permute-start | bytes 196616 | tf_op jit(solution)/shard_map/ppermute | solution.py:170
  7.8 4.7 %collective-permute-start.3 = (bf16[32,1024]{1,0:T(8,128)(2,1)S(1)}, bf16[32,1024]{1,0:T(8,128)(2,1)S(1)}, u32[]{:S(2)}, u32[]{:S(2)}) collective-permute-start(bf16[32,1024]{1,0:T(8,128)(2,1)S(1)} %get-tuple-element.31), channel_id=1, source_target_pairs={{0,28},{4,24},{8,20},{12,16},{16,12},{20,8},{24,4},{28,0},{1,29},{... | collective-permute-start | bytes 196616 | tf_op jit(solution)/shard_map/ppermute | solution.py:170
  12.5 0.0 collective-permute-start.4
  12.5 0.6 %constant_dynamic-slice_fusion.8 = s32[1,1]{0,1:T(1,128)} fusion(s32[4,1]{0,1:T(1,128)S(1)} %copy-done, s32[]{:T(128)S(6)} %select_n.35), kind=kLoop, calls=%fused_computation.16 | loop fusion | bytes 12 | tf_op jit(solution)/shard_map/dynamic_slice | solution.py:177
  13.1 0.0 collective-permute-done.refs_1_
  13.1 0.8 %collective-permute-start.5 = (bf16[32,1024]{1,0:T(8,128)(2,1)S(1)}, bf16[32,1024]{1,0:T(8,128)(2,1)S(1)}, u32[]{:S(2)}, u32[]{:S(2)}) collective-permute-start(bf16[32,1024]{1,0:T(8,128)(2,1)S(1)} %get-tuple-element.36), channel_id=1, source_target_pairs={{0,16},{4,20},{8,24},{12,28},{16,0},{20,4},{24,8},{28,12},{1,17},{... | collective-permute-start | bytes 196616 | tf_op jit(solution)/shard_map/ppermute | solution.py:170
  13.9 0.0 collective-permute-done.1.refs_2_
  13.9 1.4 %collective-permute-start.6 = (bf16[32,1024]{1,0:T(8,128)(2,1)S(1)}, bf16[32,1024]{1,0:T(8,128)(2,1)S(1)}, u32[]{:S(2)}, u32[]{:S(2)}) collective-permute-start(bf16[32,1024]{1,0:T(8,128)(2,1)S(1)} %get-tuple-element.29), channel_id=1, source_target_pairs={{0,4},{4,0},{8,12},{12,8},{16,20},{20,16},{24,28},{28,24},{1,5},{5... | collective-permute-start | bytes 196616 | tf_op jit(solution)/shard_map/ppermute | solution.py:170
  15.3 2.0 %shard_map.55 = (bf16[128,4096]{1,0:T(8,128)(2,1)S(1)}, s32[8,512]{1,0:T(8,128)S(1)}, f32[8,512]{1,0:T(8,128)S(1)}, f32[8,512]{1,0:T(8,128)S(1)}) custom-call(s32[1]{0:T(128)} %bitcast.count_ref, s32[8,512]{1,0:T(8,128)S(1)} %bitcast.4, f32[8,512]{1,0:T(8,128)S(1)} %bitcast.5, bf16[8,512]{1,0:T(8,128)(2,1)S(1)} %bitcast.6, ...), custom_call_target="tpu_custom_call" | custom-call | flops 1073741824 | bytes 1048576 | tf_op jit(solution)/shard_map/pallas_call | solution.py:129
  17.3 0.0 collective-permute-done.4.refs_5_
  17.3 1.0 %collective-permute-done.5.refs_6_ = bf16[32,1024]{1,0:T(8,128)(2,1)S(1)} collective-permute-done((bf16[32,1024]{1,0:T(8,128)(2,1)S(1)}, bf16[32,1024]{1,0:T(8,128)(2,1)S(1)}, u32[]{:S(2)}, u32[]{:S(2)}) %collective-permute-start.5) | collective-permute-done | bytes 65568 | tf_op jit(solution)/shard_map/ppermute | solution.py:170
  18.3 7.3 %shard_map.56 = (bf16[32,1024]{1,0:T(8,128)(2,1)S(1)}, bf16[32,1024]{1,0:T(8,128)(2,1)S(1)}, bf16[32,1024]{1,0:T(8,128)(2,1)S(1)}, bf16[32,1024]{1,0:T(8,128)(2,...) custom-call(s32[8,512]{1,0:T(8,128)S(1)} %get-tuple-element.17.index, ...), custom_call_target="tpu_custom_call" | custom-call | tf_op jit(solution)/shard_map/pallas_call | solution.py:145
  25.6 3.5 %collective-permute-start.7 = (bf16[32,1024]{1,0:T(8,128)(2,1)S(1)}, bf16[32,1024]{1,0:T(8,128)(2,1)S(1)}, u32[]{:S(2)}, u32[]{:S(2)}) collective-permute-start(bf16[32,1024]{1,0:T(8,128)(2,1)S(1)} %get-tuple-element.22), channel_id=1, source_target_pairs={{0,28},{4,24},{8,20},{12,16},{16,12},{20,8},{24,4},{28,0},{1,29},{... | collective-permute-start | bytes 196616 | tf_op jit(solution)/shard_map/ppermute | solution.py:170
  29.1 0.9 %collective-permute-start.8 = (bf16[32,1024]{1,0:T(8,128)(2,1)S(1)}, bf16[32,1024]{1,0:T(8,128)(2,1)S(1)}, u32[]{:S(2)}, u32[]{:S(2)}) collective-permute-start(bf16[32,1024]{1,0:T(8,128)(2,1)S(1)} %get-tuple-element.23), channel_id=1, source_target_pairs={{0,20},{4,16},{8,28},{12,24},{16,4},{20,0},{24,12},{28,8},{1,21},{... | collective-permute-start | bytes 196616 | tf_op jit(solution)/shard_map/ppermute | solution.py:170
  30.0 1.5 %collective-permute-start.9 = (bf16[32,1024]{1,0:T(8,128)(2,1)S(1)}, bf16[32,1024]{1,0:T(8,128)(2,1)S(1)}, u32[]{:S(2)}, u32[]{:S(2)}) collective-permute-start(bf16[32,1024]{1,0:T(8,128)(2,1)S(1)} %get-tuple-element.24), channel_id=1, source_target_pairs={{0,24},{4,28},{8,16},{12,20},{16,8},{20,12},{24,0},{28,4},{1,25},{... | collective-permute-start | bytes 196616 | tf_op jit(solution)/shard_map/ppermute | solution.py:170
  31.5 2.0 %collective-permute-start.10 = (bf16[32,1024]{1,0:T(8,128)(2,1)S(1)}, bf16[32,1024]{1,0:T(8,128)(2,1)S(1)}, u32[]{:S(2)}, u32[]{:S(2)}) collective-permute-start(bf16[32,1024]{1,0:T(8,128)(2,1)S(1)} %get-tuple-element.25), channel_id=1, source_target_pairs={{0,12},{4,8},{8,4},{12,0},{16,28},{20,24},{24,20},{28,16},{1,13},{... | collective-permute-start | bytes 196616 | tf_op jit(solution)/shard_map/ppermute | solution.py:170
  33.5 0.0 collective-permute-start.11
  33.6 0.0 collective-permute-done.7
  33.6 2.3 %collective-permute-start.12 = (bf16[32,1024]{1,0:T(8,128)(2,1)S(1)}, bf16[32,1024]{1,0:T(8,128)(2,1)S(1)}, u32[]{:S(2)}, u32[]{:S(2)}) collective-permute-start(bf16[32,1024]{1,0:T(8,128)(2,1)S(1)} %get-tuple-element.27), channel_id=1, source_target_pairs={{0,16},{4,20},{8,24},{12,28},{16,0},{20,4},{24,8},{28,12},{1,17},{... | collective-permute-start | bytes 196616 | tf_op jit(solution)/shard_map/ppermute | solution.py:170
  35.9 1.9 %collective-permute-done.8 = bf16[32,1024]{1,0:T(8,128)(2,1)S(1)} collective-permute-done((bf16[32,1024]{1,0:T(8,128)(2,1)S(1)}, bf16[32,1024]{1,0:T(8,128)(2,1)S(1)}, u32[]{:S(2)}, u32[]{:S(2)}) %collective-permute-start.8) | collective-permute-done | bytes 65568 | tf_op jit(solution)/shard_map/ppermute | solution.py:170
  37.8 1.0 %collective-permute-start.13 = (bf16[32,1024]{1,0:T(8,128)(2,1)S(1)}, bf16[32,1024]{1,0:T(8,128)(2,1)S(1)}, u32[]{:S(2)}, u32[]{:S(2)}) collective-permute-start(bf16[32,1024]{1,0:T(8,128)(2,1)S(1)} %get-tuple-element.28), channel_id=1, source_target_pairs={{0,4},{4,0},{8,12},{12,8},{16,20},{20,16},{24,28},{28,24},{1,5},{5... | collective-permute-start | bytes 196616 | tf_op jit(solution)/shard_map/ppermute | solution.py:170
  38.8 0.0 collective-permute-done.9
  38.8 0.0 collective-permute-done.10
  38.9 0.2 collective-permute-done.12
  39.1 0.0 copy-start.4
  39.1 2.9 %collective-permute-done.13 = bf16[32,1024]{1,0:T(8,128)(2,1)S(1)} collective-permute-done((bf16[32,1024]{1,0:T(8,128)(2,1)S(1)}, bf16[32,1024]{1,0:T(8,128)(2,1)S(1)}, u32[]{:S(2)}, u32[]{:S(2)}) %collective-permute-start.13) | collective-permute-done | bytes 65568 | tf_op jit(solution)/shard_map/ppermute | solution.py:170
  42.1 0.6 %constant_dynamic-update-slice_fusion = bf16[32,8192]{1,0:T(8,128)(2,1)} fusion(bf16[32,8192]{1,0:T(8,128)(2,1)} %copy-done.4, bf16[32,1024]{1,0:T(8,128)(2,1)S(1)} %collective-permute-done.13, s32[]{:T(128)S(6)} %select_n.43), kind=kLoop, calls=%fused_computation | loop fusion | bytes 131076 | tf_op jit(solution)/shard_map/dynamic_update_slice | solution.py:193
  (19 shorter events, 0.1 us)
Async XLA Ops:
  0.0 12.5 %copy-start = (s32[4,1]{0,1:T(1,128)S(1)}, s32[4,1]{0,1:T(1,128)}, u32[]{:S(2)}) copy-start(s32[4,1]{0,1:T(1,128)} %param.6) | copy-start | bytes 52
  0.0 15.3 %copy-start.3 = (bf16[1,1,8,512]{3,2,1,0:T(8,128)(2,1)S(1)}, bf16[1,1,8,512]{3,2,1,0:T(8,128)(2,1)}, u32[]{:S(2)}) copy-start(bf16[1,1,8,512]{3,2,1,0:T(8,128)(2,1)} %param.9) | copy-start | bytes 24580
  1.1 14.1 %copy-start.1 = (s32[1,1,8,512]{3,2,1,0:T(8,128)S(1)}, s32[1,1,8,512]{3,2,1,0:T(8,128)}, u32[]{:S(2)}) copy-start(s32[1,1,8,512]{3,2,1,0:T(8,128)} %param.7) | copy-start | bytes 49156
  1.1 14.1 %copy-start.2 = (f32[1,1,8,512]{3,2,1,0:T(8,128)S(1)}, f32[1,1,8,512]{3,2,1,0:T(8,128)}, u32[]{:S(2)}) copy-start(f32[1,1,8,512]{3,2,1,0:T(8,128)} %param.8) | copy-start | bytes 49156
  1.2 11.9 %collective-permute-start = (bf16[32,1024]{1,0:T(8,128)(2,1)S(1)}, bf16[32,1024]{1,0:T(8,128)(2,1)S(1)}, u32[]{:S(2)}, u32[]{:S(2)}) collective-permute-start(bf16[32,1024]{1,0:T(8,128)(2,1)S(1)} %get-tuple-element.34), channel_id=1, source_target_pairs={{0,24},{4,28},{8,16},{12,20},{16,8},{20,12},{24,0},{28,4},{1,25},{... | collective-permute-start | bytes 196616 | tf_op jit(solution)/shard_map/ppermute | solution.py:170
  6.3 7.6 %collective-permute-start.1 = (bf16[32,1024]{1,0:T(8,128)(2,1)S(1)}, bf16[32,1024]{1,0:T(8,128)(2,1)S(1)}, u32[]{:S(2)}, u32[]{:S(2)}) collective-permute-start(bf16[32,1024]{1,0:T(8,128)(2,1)S(1)} %get-tuple-element.33), channel_id=1, source_target_pairs={{0,20},{4,16},{8,28},{12,24},{16,4},{20,0},{24,12},{28,8},{1,21},{... | collective-permute-start | bytes 196616 | tf_op jit(solution)/shard_map/ppermute | solution.py:170
  6.7 8.6 %collective-permute-start.2 = (bf16[32,1024]{1,0:T(8,128)(2,1)S(1)}, bf16[32,1024]{1,0:T(8,128)(2,1)S(1)}, u32[]{:S(2)}, u32[]{:S(2)}) collective-permute-start(bf16[32,1024]{1,0:T(8,128)(2,1)S(1)} %get-tuple-element.32), channel_id=1, source_target_pairs={{0,12},{4,8},{8,4},{12,0},{16,28},{20,24},{24,20},{28,16},{1,13},{... | collective-permute-start | bytes 196616 | tf_op jit(solution)/shard_map/ppermute | solution.py:170
  7.8 9.4 %collective-permute-start.3 = (bf16[32,1024]{1,0:T(8,128)(2,1)S(1)}, bf16[32,1024]{1,0:T(8,128)(2,1)S(1)}, u32[]{:S(2)}, u32[]{:S(2)}) collective-permute-start(bf16[32,1024]{1,0:T(8,128)(2,1)S(1)} %get-tuple-element.31), channel_id=1, source_target_pairs={{0,28},{4,24},{8,20},{12,16},{16,12},{20,8},{24,4},{28,0},{1,29},{... | collective-permute-start | bytes 196616 | tf_op jit(solution)/shard_map/ppermute | solution.py:170
  12.5 4.8 %collective-permute-start.4 = (bf16[32,1024]{1,0:T(8,128)(2,1)S(1)}, bf16[32,1024]{1,0:T(8,128)(2,1)S(1)}, u32[]{:S(2)}, u32[]{:S(2)}) collective-permute-start(bf16[32,1024]{1,0:T(8,128)(2,1)S(1)} %get-tuple-element.30), channel_id=1, source_target_pairs={{0,8},{4,12},{8,0},{12,4},{16,24},{20,28},{24,16},{28,20},{1,9},{5... | collective-permute-start | bytes 196616 | tf_op jit(solution)/shard_map/ppermute | solution.py:170
  13.1 5.2 %collective-permute-start.5 = (bf16[32,1024]{1,0:T(8,128)(2,1)S(1)}, bf16[32,1024]{1,0:T(8,128)(2,1)S(1)}, u32[]{:S(2)}, u32[]{:S(2)}) collective-permute-start(bf16[32,1024]{1,0:T(8,128)(2,1)S(1)} %get-tuple-element.36), channel_id=1, source_target_pairs={{0,16},{4,20},{8,24},{12,28},{16,0},{20,4},{24,8},{28,12},{1,17},{... | collective-permute-start | bytes 196616 | tf_op jit(solution)/shard_map/ppermute | solution.py:170
  13.9 4.4 %collective-permute-start.6 = (bf16[32,1024]{1,0:T(8,128)(2,1)S(1)}, bf16[32,1024]{1,0:T(8,128)(2,1)S(1)}, u32[]{:S(2)}, u32[]{:S(2)}) collective-permute-start(bf16[32,1024]{1,0:T(8,128)(2,1)S(1)} %get-tuple-element.29), channel_id=1, source_target_pairs={{0,4},{4,0},{8,12},{12,8},{16,20},{20,16},{24,28},{28,24},{1,5},{5... | collective-permute-start | bytes 196616 | tf_op jit(solution)/shard_map/ppermute | solution.py:170
  25.6 8.0 %collective-permute-start.7 = (bf16[32,1024]{1,0:T(8,128)(2,1)S(1)}, bf16[32,1024]{1,0:T(8,128)(2,1)S(1)}, u32[]{:S(2)}, u32[]{:S(2)}) collective-permute-start(bf16[32,1024]{1,0:T(8,128)(2,1)S(1)} %get-tuple-element.22), channel_id=1, source_target_pairs={{0,28},{4,24},{8,20},{12,16},{16,12},{20,8},{24,4},{28,0},{1,29},{... | collective-permute-start | bytes 196616 | tf_op jit(solution)/shard_map/ppermute | solution.py:170
  29.1 8.7 %collective-permute-start.8 = (bf16[32,1024]{1,0:T(8,128)(2,1)S(1)}, bf16[32,1024]{1,0:T(8,128)(2,1)S(1)}, u32[]{:S(2)}, u32[]{:S(2)}) collective-permute-start(bf16[32,1024]{1,0:T(8,128)(2,1)S(1)} %get-tuple-element.23), channel_id=1, source_target_pairs={{0,20},{4,16},{8,28},{12,24},{16,4},{20,0},{24,12},{28,8},{1,21},{... | collective-permute-start | bytes 196616 | tf_op jit(solution)/shard_map/ppermute | solution.py:170
  30.0 8.8 %collective-permute-start.9 = (bf16[32,1024]{1,0:T(8,128)(2,1)S(1)}, bf16[32,1024]{1,0:T(8,128)(2,1)S(1)}, u32[]{:S(2)}, u32[]{:S(2)}) collective-permute-start(bf16[32,1024]{1,0:T(8,128)(2,1)S(1)} %get-tuple-element.24), channel_id=1, source_target_pairs={{0,24},{4,28},{8,16},{12,20},{16,8},{20,12},{24,0},{28,4},{1,25},{... | collective-permute-start | bytes 196616 | tf_op jit(solution)/shard_map/ppermute | solution.py:170
  31.5 7.3 %collective-permute-start.10 = (bf16[32,1024]{1,0:T(8,128)(2,1)S(1)}, bf16[32,1024]{1,0:T(8,128)(2,1)S(1)}, u32[]{:S(2)}, u32[]{:S(2)}) collective-permute-start(bf16[32,1024]{1,0:T(8,128)(2,1)S(1)} %get-tuple-element.25), channel_id=1, source_target_pairs={{0,12},{4,8},{8,4},{12,0},{16,28},{20,24},{24,20},{28,16},{1,13},{... | collective-permute-start | bytes 196616 | tf_op jit(solution)/shard_map/ppermute | solution.py:170
  33.5 5.4 %collective-permute-start.11 = (bf16[32,1024]{1,0:T(8,128)(2,1)S(1)}, bf16[32,1024]{1,0:T(8,128)(2,1)S(1)}, u32[]{:S(2)}, u32[]{:S(2)}) collective-permute-start(bf16[32,1024]{1,0:T(8,128)(2,1)S(1)} %get-tuple-element.26), channel_id=1, source_target_pairs={{0,8},{4,12},{8,0},{12,4},{16,24},{20,28},{24,16},{28,20},{1,9},{5... | collective-permute-start | bytes 196616 | tf_op jit(solution)/shard_map/ppermute | solution.py:170
  33.6 5.5 %collective-permute-start.12 = (bf16[32,1024]{1,0:T(8,128)(2,1)S(1)}, bf16[32,1024]{1,0:T(8,128)(2,1)S(1)}, u32[]{:S(2)}, u32[]{:S(2)}) collective-permute-start(bf16[32,1024]{1,0:T(8,128)(2,1)S(1)} %get-tuple-element.27), channel_id=1, source_target_pairs={{0,16},{4,20},{8,24},{12,28},{16,0},{20,4},{24,8},{28,12},{1,17},{... | collective-permute-start | bytes 196616 | tf_op jit(solution)/shard_map/ppermute | solution.py:170
  37.8 4.3 %collective-permute-start.13 = (bf16[32,1024]{1,0:T(8,128)(2,1)S(1)}, bf16[32,1024]{1,0:T(8,128)(2,1)S(1)}, u32[]{:S(2)}, u32[]{:S(2)}) collective-permute-start(bf16[32,1024]{1,0:T(8,128)(2,1)S(1)} %get-tuple-element.28), channel_id=1, source_target_pairs={{0,4},{4,0},{8,12},{12,8},{16,20},{20,16},{24,28},{28,24},{1,5},{5... | collective-permute-start | bytes 196616 | tf_op jit(solution)/shard_map/ppermute | solution.py:170
  39.1 3.0 %copy-start.4 = (bf16[32,8192]{1,0:T(8,128)(2,1)}, bf16[32,8192]{1,0:T(8,128)(2,1)S(1)}, u32[]{:S(2)}) copy-start(bf16[32,8192]{1,0:T(8,128)(2,1)S(1)} %constant_dynamic-update-slice_fusion.1) | copy-start | bytes 1572868

commit v5 on v4

--- a/solution.py
+++ b/solution.py
@@ -49,13 +49,22 @@
         picked_ref[:, block * nobs : (block + 1) * nobs] = picked.astype(BF16)
 
 
+def add_diagonal(matrix, eye, value):
+    size, tile = matrix.shape[0], eye.shape[0]
+    rows = []
+    for i in range(0, size, tile):
+        cells = [matrix[i : i + tile, j : j + tile] for j in range(0, size, tile)]
+        rows.append(jnp.concatenate([c + value * eye if k * tile == i else c for k, c in enumerate(cells)], axis=1))
+    return jnp.concatenate(rows, axis=0)
+
+
 def newton_steps(iterates, eye):
     roots = [None] * len(iterates)
     for step in range(NS_ITERS):
         if step == 0:
-            factors = [(1.5 * eye).astype(BF16) - BF16(0.5) * y for y in iterates]
+            factors = [add_diagonal(BF16(-0.5) * y, eye.astype(BF16), BF16(1.5)) for y in iterates]
         else:
-            factors = [(1.5 * eye - 0.5 * dot(r, y)).astype(BF16) for r, y in zip(roots, iterates)]
+            factors = [add_diagonal(-0.5 * dot(r, y), eye, 1.5).astype(BF16) for r, y in zip(roots, iterates)]
         if step < NS_ITERS - 1:
             iterates = [dot(y, f).astype(BF16) for y, f in zip(iterates, factors)]
         roots = factors if step == 0 else [dot(f, r).astype(BF16) for f, r in zip(factors, roots)]
@@ -75,7 +84,8 @@
         anomaly_s[p * share : (p + 1) * share, :] = (ref[...].astype(F32) - mean).astype(BF16)
     for j in range(slots):
         mean_s[j : j + 1, :] = mean[:, j * width : (j + 1) * width]
-    square = (members, members)
+    tile = 128 if members % 128 == 0 else members
+    square = (tile, tile)
     eye = (lax.broadcasted_iota(jnp.int32, square, 0) == lax.broadcasted_iota(jnp.int32, square, 1)).astype(F32)
     high = mean.astype(BF16).astype(F32)
     middle = (mean - high).astype(BF16).astype(F32)
@@ -105,7 +115,7 @@
     rights = [p[members : members + 1] for p in products]
     iterates, scales = [], []
     for block in blocks:
-        gram = products[block][:members] + (members - 1.0) * eye
+        gram = add_diagonal(products[block][:members], eye, members - 1.0)
         scale = jnp.sqrt(jnp.sum(jnp.sum(gram * gram, axis=0, keepdims=True), axis=1, keepdims=True))
         scales.append(scale)
         iterates.append((gram * (1.0 / scale)).astype(BF16))

time: 42.9 us -> 42.9 us (level)
  no operation moved by 1% of the time
where the time goes in v5:
time: 42.9 us; the launch traced here: 42.7 us
  starting transfers between devices  24.7 us (58%)
  Pallas kernels  9.28 us (22%)
  waiting for transfers between devices  6.09 us (14%)
  local copies, waits for them, and re-layouts  2.48 us (6%)
    ppermute x14, starting transfers between devices, exchange(): lax.ppermute(block, 'wide', [(i, i ^ step) for i in range(lax.axis_size('...  24.7 us
    pallas_call x1, Pallas kernels, analyse(): pl.pallas_call(functools.partial(main_kernel, parts, early), out_shape=[j...  7.28 us
    ppermute x14, waiting for transfers between devices, exchange(): lax.ppermute(block, 'wide', [(i, i ^ step) for i in range(lax.axis_size('...  6.09 us
    pallas_call x1, Pallas kernels, analyse(): pl.pallas_call(functools.partial(early_kernel, early), out_shape=[jax.Sha...  2 us
    dynamic_slice x1, local copies, waits for them, and re-layouts, per_device(): lax.dynamic_slice(fields, (0, (me ^ s) * cells), (share, cells))  1.12 us
  transfers between devices with their start and end apart: 14, of which 4 were waited for; matrix products, arithmetic and copies ran while one was open for 2% of the time, Pallas kernels for 5%

profile of v5, /device:TPU:0, one launch (start us, length us, event | category | flops | bytes accessed | tf_op | source)
XLA Modules:
  0.0 42.7 jit_solution(9684234008239294121)
XLA Ops:
  0.0 1.1 %constant_dynamic-slice_fusion = (bf16[32,1024]{1,0:T(8,128)(2,1)S(1)}, bf16[32,1024]{1,0:T(8,128)(2,1)S(1)}, bf16[32,1024]{1,0:T(8,128)(2,1)S(1)}, bf16[32,1024...) fusion(bf16[32,8192]{1,0:T(8,128)(2,1)} %param.5, ...), kind=kLoop, calls=%fused_computation.8 | loop fusion | bytes 1048608 | tf_op jit(solution)/shard_map/dynamic_slice | solution.py:196
  1.1 0.0 copy-start.1
  1.1 0.0 copy-start.2
  1.2 5.1 %collective-permute-start = (bf16[32,1024]{1,0:T(8,128)(2,1)S(1)}, bf16[32,1024]{1,0:T(8,128)(2,1)S(1)}, u32[]{:S(2)}, u32[]{:S(2)}) collective-permute-start(bf16[32,1024]{1,0:T(8,128)(2,1)S(1)} %get-tuple-element.34), channel_id=1, source_target_pairs={{0,24},{4,28},{8,16},{12,20},{16,8},{20,12},{24,0},{28,4},{1,25},{... | collective-permute-start | bytes 196616 | tf_op jit(solution)/shard_map/ppermute | solution.py:180
  6.3 0.4 collective-permute-start.1
  6.7 1.2 %collective-permute-start.2 = (bf16[32,1024]{1,0:T(8,128)(2,1)S(1)}, bf16[32,1024]{1,0:T(8,128)(2,1)S(1)}, u32[]{:S(2)}, u32[]{:S(2)}) collective-permute-start(bf16[32,1024]{1,0:T(8,128)(2,1)S(1)} %get-tuple-element.32), channel_id=1, source_target_pairs={{0,12},{4,8},{8,4},{12,0},{16,28},{20,24},{24,20},{28,16},{1,13},{... | collective-permute-start | bytes 196616 | tf_op jit(solution)/shard_map/ppermute | solution.py:180
  7.8 4.7 %collective-permute-start.3 = (bf16[32,1024]{1,0:T(8,128)(2,1)S(1)}, bf16[32,1024]{1,0:T(8,128)(2,1)S(1)}, u32[]{:S(2)}, u32[]{:S(2)}) collective-permute-start(bf16[32,1024]{1,0:T(8,128)(2,1)S(1)} %get-tuple-element.31), channel_id=1, source_target_pairs={{0,28},{4,24},{8,20},{12,16},{16,12},{20,8},{24,4},{28,0},{1,29},{... | collective-permute-start | bytes 196616 | tf_op jit(solution)/shard_map/ppermute | solution.py:180
  12.5 0.0 collective-permute-start.4
  12.5 0.6 %constant_dynamic-slice_fusion.8 = s32[1,1]{0,1:T(1,128)} fusion(s32[4,1]{0,1:T(1,128)S(1)} %copy-done, s32[]{:T(128)S(6)} %select_n.35), kind=kLoop, calls=%fused_computation.16 | loop fusion | bytes 12 | tf_op jit(solution)/shard_map/dynamic_slice | solution.py:187
  13.1 0.0 collective-permute-done.refs_1_
  13.1 0.8 %collective-permute-start.5 = (bf16[32,1024]{1,0:T(8,128)(2,1)S(1)}, bf16[32,1024]{1,0:T(8,128)(2,1)S(1)}, u32[]{:S(2)}, u32[]{:S(2)}) collective-permute-start(bf16[32,1024]{1,0:T(8,128)(2,1)S(1)} %get-tuple-element.36), channel_id=1, source_target_pairs={{0,16},{4,20},{8,24},{12,28},{16,0},{20,4},{24,8},{28,12},{1,17},{... | collective-permute-start | bytes 196616 | tf_op jit(solution)/shard_map/ppermute | solution.py:180
  13.9 0.0 collective-permute-done.1.refs_2_
  13.9 1.4 %collective-permute-start.6 = (bf16[32,1024]{1,0:T(8,128)(2,1)S(1)}, bf16[32,1024]{1,0:T(8,128)(2,1)S(1)}, u32[]{:S(2)}, u32[]{:S(2)}) collective-permute-start(bf16[32,1024]{1,0:T(8,128)(2,1)S(1)} %get-tuple-element.29), channel_id=1, source_target_pairs={{0,4},{4,0},{8,12},{12,8},{16,20},{20,16},{24,28},{28,24},{1,5},{5... | collective-permute-start | bytes 196616 | tf_op jit(solution)/shard_map/ppermute | solution.py:180
  15.2 0.0 collective-permute-done.2.refs_3_
  15.3 2.0 %shard_map.55 = (bf16[128,4096]{1,0:T(8,128)(2,1)S(1)}, s32[8,512]{1,0:T(8,128)S(1)}, f32[8,512]{1,0:T(8,128)S(1)}, f32[8,512]{1,0:T(8,128)S(1)}) custom-call(s32[1]{0:T(128)} %bitcast.count_ref, s32[8,512]{1,0:T(8,128)S(1)} %bitcast.4, f32[8,512]{1,0:T(8,128)S(1)} %bitcast.5, bf16[8,512]{1,0:T(8,128)(2,1)S(1)} %bitcast.6, ...), custom_call_target="tpu_custom_call" | custom-call | flops 1073741824 | bytes 1048576 | tf_op jit(solution)/shard_map/pallas_call | solution.py:139
  17.3 0.0 collective-permute-done.4.refs_5_
  17.3 1.0 %collective-permute-done.5.refs_6_ = bf16[32,1024]{1,0:T(8,128)(2,1)S(1)} collective-permute-done((bf16[32,1024]{1,0:T(8,128)(2,1)S(1)}, bf16[32,1024]{1,0:T(8,128)(2,1)S(1)}, u32[]{:S(2)}, u32[]{:S(2)}) %collective-permute-start.5) | collective-permute-done | bytes 65568 | tf_op jit(solution)/shard_map/ppermute | solution.py:180
  18.3 7.3 %shard_map.56 = (bf16[32,1024]{1,0:T(8,128)(2,1)S(1)}, bf16[32,1024]{1,0:T(8,128)(2,1)S(1)}, bf16[32,1024]{1,0:T(8,128)(2,1)S(1)}, bf16[32,1024]{1,0:T(8,128)(2,...) custom-call(s32[8,512]{1,0:T(8,128)S(1)} %get-tuple-element.17.index, ...), custom_call_target="tpu_custom_call" | custom-call | tf_op jit(solution)/shard_map/pallas_call | solution.py:155
  25.6 3.5 %collective-permute-start.7 = (bf16[32,1024]{1,0:T(8,128)(2,1)S(1)}, bf16[32,1024]{1,0:T(8,128)(2,1)S(1)}, u32[]{:S(2)}, u32[]{:S(2)}) collective-permute-start(bf16[32,1024]{1,0:T(8,128)(2,1)S(1)} %get-tuple-element.22), channel_id=1, source_target_pairs={{0,28},{4,24},{8,20},{12,16},{16,12},{20,8},{24,4},{28,0},{1,29},{... | collective-permute-start | bytes 196616 | tf_op jit(solution)/shard_map/ppermute | solution.py:180
  29.1 0.9 %collective-permute-start.8 = (bf16[32,1024]{1,0:T(8,128)(2,1)S(1)}, bf16[32,1024]{1,0:T(8,128)(2,1)S(1)}, u32[]{:S(2)}, u32[]{:S(2)}) collective-permute-start(bf16[32,1024]{1,0:T(8,128)(2,1)S(1)} %get-tuple-element.23), channel_id=1, source_target_pairs={{0,20},{4,16},{8,28},{12,24},{16,4},{20,0},{24,12},{28,8},{1,21},{... | collective-permute-start | bytes 196616 | tf_op jit(solution)/shard_map/ppermute | solution.py:180
  30.0 1.5 %collective-permute-start.9 = (bf16[32,1024]{1,0:T(8,128)(2,1)S(1)}, bf16[32,1024]{1,0:T(8,128)(2,1)S(1)}, u32[]{:S(2)}, u32[]{:S(2)}) collective-permute-start(bf16[32,1024]{1,0:T(8,128)(2,1)S(1)} %get-tuple-element.24), channel_id=1, source_target_pairs={{0,24},{4,28},{8,16},{12,20},{16,8},{20,12},{24,0},{28,4},{1,25},{... | collective-permute-start | bytes 196616 | tf_op jit(solution)/shard_map/ppermute | solution.py:180
  31.5 2.0 %collective-permute-start.10 = (bf16[32,1024]{1,0:T(8,128)(2,1)S(1)}, bf16[32,1024]{1,0:T(8,128)(2,1)S(1)}, u32[]{:S(2)}, u32[]{:S(2)}) collective-permute-start(bf16[32,1024]{1,0:T(8,128)(2,1)S(1)} %get-tuple-element.25), channel_id=1, source_target_pairs={{0,12},{4,8},{8,4},{12,0},{16,28},{20,24},{24,20},{28,16},{1,13},{... | collective-permute-start | bytes 196616 | tf_op jit(solution)/shard_map/ppermute | solution.py:180
  33.5 0.0 collective-permute-start.11
  33.6 2.3 %collective-permute-start.12 = (bf16[32,1024]{1,0:T(8,128)(2,1)S(1)}, bf16[32,1024]{1,0:T(8,128)(2,1)S(1)}, u32[]{:S(2)}, u32[]{:S(2)}) collective-permute-start(bf16[32,1024]{1,0:T(8,128)(2,1)S(1)} %get-tuple-element.27), channel_id=1, source_target_pairs={{0,16},{4,20},{8,24},{12,28},{16,0},{20,4},{24,8},{28,12},{1,17},{... | collective-permute-start | bytes 196616 | tf_op jit(solution)/shard_map/ppermute | solution.py:180
  35.9 1.9 %collective-permute-done.8 = bf16[32,1024]{1,0:T(8,128)(2,1)S(1)} collective-permute-done((bf16[32,1024]{1,0:T(8,128)(2,1)S(1)}, bf16[32,1024]{1,0:T(8,128)(2,1)S(1)}, u32[]{:S(2)}, u32[]{:S(2)}) %collective-permute-start.8) | collective-permute-done | bytes 65568 | tf_op jit(solution)/shard_map/ppermute | solution.py:180
  37.8 1.0 %collective-permute-start.13 = (bf16[32,1024]{1,0:T(8,128)(2,1)S(1)}, bf16[32,1024]{1,0:T(8,128)(2,1)S(1)}, u32[]{:S(2)}, u32[]{:S(2)}) collective-permute-start(bf16[32,1024]{1,0:T(8,128)(2,1)S(1)} %get-tuple-element.28), channel_id=1, source_target_pairs={{0,4},{4,0},{8,12},{12,8},{16,20},{20,16},{24,28},{28,24},{1,5},{5... | collective-permute-start | bytes 196616 | tf_op jit(solution)/shard_map/ppermute | solution.py:180
  38.8 0.0 collective-permute-done.9
  38.8 0.0 collective-permute-done.11
  38.9 0.2 collective-permute-done.12
  39.1 0.0 copy-start.4
  39.1 2.9 %collective-permute-done.13 = bf16[32,1024]{1,0:T(8,128)(2,1)S(1)} collective-permute-done((bf16[32,1024]{1,0:T(8,128)(2,1)S(1)}, bf16[32,1024]{1,0:T(8,128)(2,1)S(1)}, u32[]{:S(2)}, u32[]{:S(2)}) %collective-permute-start.13) | collective-permute-done | bytes 65568 | tf_op jit(solution)/shard_map/ppermute | solution.py:180
  42.1 0.6 %constant_dynamic-update-slice_fusion = bf16[32,8192]{1,0:T(8,128)(2,1)} fusion(bf16[32,8192]{1,0:T(8,128)(2,1)} %copy-done.4, bf16[32,1024]{1,0:T(8,128)(2,1)S(1)} %collective-permute-done.13, s32[]{:T(128)S(6)} %select_n.43), kind=kLoop, calls=%fused_computation | loop fusion | bytes 131076 | tf_op jit(solution)/shard_map/dynamic_update_slice | solution.py:203
  (19 shorter events, 0.1 us)
Async XLA Ops:
  0.0 12.5 %copy-start = (s32[4,1]{0,1:T(1,128)S(1)}, s32[4,1]{0,1:T(1,128)}, u32[]{:S(2)}) copy-start(s32[4,1]{0,1:T(1,128)} %param.6) | copy-start | bytes 52
  0.0 15.3 %copy-start.3 = (bf16[1,1,8,512]{3,2,1,0:T(8,128)(2,1)S(1)}, bf16[1,1,8,512]{3,2,1,0:T(8,128)(2,1)}, u32[]{:S(2)}) copy-start(bf16[1,1,8,512]{3,2,1,0:T(8,128)(2,1)} %param.9) | copy-start | bytes 24580
  1.1 14.1 %copy-start.1 = (s32[1,1,8,512]{3,2,1,0:T(8,128)S(1)}, s32[1,1,8,512]{3,2,1,0:T(8,128)}, u32[]{:S(2)}) copy-start(s32[1,1,8,512]{3,2,1,0:T(8,128)} %param.7) | copy-start | bytes 49156
  1.1 14.1 %copy-start.2 = (f32[1,1,8,512]{3,2,1,0:T(8,128)S(1)}, f32[1,1,8,512]{3,2,1,0:T(8,128)}, u32[]{:S(2)}) copy-start(f32[1,1,8,512]{3,2,1,0:T(8,128)} %param.8) | copy-start | bytes 49156
  1.2 11.9 %collective-permute-start = (bf16[32,1024]{1,0:T(8,128)(2,1)S(1)}, bf16[32,1024]{1,0:T(8,128)(2,1)S(1)}, u32[]{:S(2)}, u32[]{:S(2)}) collective-permute-start(bf16[32,1024]{1,0:T(8,128)(2,1)S(1)} %get-tuple-element.34), channel_id=1, source_target_pairs={{0,24},{4,28},{8,16},{12,20},{16,8},{20,12},{24,0},{28,4},{1,25},{... | collective-permute-start | bytes 196616 | tf_op jit(solution)/shard_map/ppermute | solution.py:180
  6.3 7.6 %collective-permute-start.1 = (bf16[32,1024]{1,0:T(8,128)(2,1)S(1)}, bf16[32,1024]{1,0:T(8,128)(2,1)S(1)}, u32[]{:S(2)}, u32[]{:S(2)}) collective-permute-start(bf16[32,1024]{1,0:T(8,128)(2,1)S(1)} %get-tuple-element.33), channel_id=1, source_target_pairs={{0,20},{4,16},{8,28},{12,24},{16,4},{20,0},{24,12},{28,8},{1,21},{... | collective-permute-start | bytes 196616 | tf_op jit(solution)/shard_map/ppermute | solution.py:180
  6.7 8.6 %collective-permute-start.2 = (bf16[32,1024]{1,0:T(8,128)(2,1)S(1)}, bf16[32,1024]{1,0:T(8,128)(2,1)S(1)}, u32[]{:S(2)}, u32[]{:S(2)}) collective-permute-start(bf16[32,1024]{1,0:T(8,128)(2,1)S(1)} %get-tuple-element.32), channel_id=1, source_target_pairs={{0,12},{4,8},{8,4},{12,0},{16,28},{20,24},{24,20},{28,16},{1,13},{... | collective-permute-start | bytes 196616 | tf_op jit(solution)/shard_map/ppermute | solution.py:180
  7.8 9.4 %collective-permute-start.3 = (bf16[32,1024]{1,0:T(8,128)(2,1)S(1)}, bf16[32,1024]{1,0:T(8,128)(2,1)S(1)}, u32[]{:S(2)}, u32[]{:S(2)}) collective-permute-start(bf16[32,1024]{1,0:T(8,128)(2,1)S(1)} %get-tuple-element.31), channel_id=1, source_target_pairs={{0,28},{4,24},{8,20},{12,16},{16,12},{20,8},{24,4},{28,0},{1,29},{... | collective-permute-start | bytes 196616 | tf_op jit(solution)/shard_map/ppermute | solution.py:180
  12.5 4.8 %collective-permute-start.4 = (bf16[32,1024]{1,0:T(8,128)(2,1)S(1)}, bf16[32,1024]{1,0:T(8,128)(2,1)S(1)}, u32[]{:S(2)}, u32[]{:S(2)}) collective-permute-start(bf16[32,1024]{1,0:T(8,128)(2,1)S(1)} %get-tuple-element.30), channel_id=1, source_target_pairs={{0,8},{4,12},{8,0},{12,4},{16,24},{20,28},{24,16},{28,20},{1,9},{5... | collective-permute-start | bytes 196616 | tf_op jit(solution)/shard_map/ppermute | solution.py:180
  13.1 5.2 %collective-permute-start.5 = (bf16[32,1024]{1,0:T(8,128)(2,1)S(1)}, bf16[32,1024]{1,0:T(8,128)(2,1)S(1)}, u32[]{:S(2)}, u32[]{:S(2)}) collective-permute-start(bf16[32,1024]{1,0:T(8,128)(2,1)S(1)} %get-tuple-element.36), channel_id=1, source_target_pairs={{0,16},{4,20},{8,24},{12,28},{16,0},{20,4},{24,8},{28,12},{1,17},{... | collective-permute-start | bytes 196616 | tf_op jit(solution)/shard_map/ppermute | solution.py:180
  13.9 4.4 %collective-permute-start.6 = (bf16[32,1024]{1,0:T(8,128)(2,1)S(1)}, bf16[32,1024]{1,0:T(8,128)(2,1)S(1)}, u32[]{:S(2)}, u32[]{:S(2)}) collective-permute-start(bf16[32,1024]{1,0:T(8,128)(2,1)S(1)} %get-tuple-element.29), channel_id=1, source_target_pairs={{0,4},{4,0},{8,12},{12,8},{16,20},{20,16},{24,28},{28,24},{1,5},{5... | collective-permute-start | bytes 196616 | tf_op jit(solution)/shard_map/ppermute | solution.py:180
  25.6 8.0 %collective-permute-start.7 = (bf16[32,1024]{1,0:T(8,128)(2,1)S(1)}, bf16[32,1024]{1,0:T(8,128)(2,1)S(1)}, u32[]{:S(2)}, u32[]{:S(2)}) collective-permute-start(bf16[32,1024]{1,0:T(8,128)(2,1)S(1)} %get-tuple-element.22), channel_id=1, source_target_pairs={{0,28},{4,24},{8,20},{12,16},{16,12},{20,8},{24,4},{28,0},{1,29},{... | collective-permute-start | bytes 196616 | tf_op jit(solution)/shard_map/ppermute | solution.py:180
  29.1 8.7 %collective-permute-start.8 = (bf16[32,1024]{1,0:T(8,128)(2,1)S(1)}, bf16[32,1024]{1,0:T(8,128)(2,1)S(1)}, u32[]{:S(2)}, u32[]{:S(2)}) collective-permute-start(bf16[32,1024]{1,0:T(8,128)(2,1)S(1)} %get-tuple-element.23), channel_id=1, source_target_pairs={{0,20},{4,16},{8,28},{12,24},{16,4},{20,0},{24,12},{28,8},{1,21},{... | collective-permute-start | bytes 196616 | tf_op jit(solution)/shard_map/ppermute | solution.py:180
  30.0 8.8 %collective-permute-start.9 = (bf16[32,1024]{1,0:T(8,128)(2,1)S(1)}, bf16[32,1024]{1,0:T(8,128)(2,1)S(1)}, u32[]{:S(2)}, u32[]{:S(2)}) collective-permute-start(bf16[32,1024]{1,0:T(8,128)(2,1)S(1)} %get-tuple-element.24), channel_id=1, source_target_pairs={{0,24},{4,28},{8,16},{12,20},{16,8},{20,12},{24,0},{28,4},{1,25},{... | collective-permute-start | bytes 196616 | tf_op jit(solution)/shard_map/ppermute | solution.py:180
  31.5 7.3 %collective-permute-start.10 = (bf16[32,1024]{1,0:T(8,128)(2,1)S(1)}, bf16[32,1024]{1,0:T(8,128)(2,1)S(1)}, u32[]{:S(2)}, u32[]{:S(2)}) collective-permute-start(bf16[32,1024]{1,0:T(8,128)(2,1)S(1)} %get-tuple-element.25), channel_id=1, source_target_pairs={{0,12},{4,8},{8,4},{12,0},{16,28},{20,24},{24,20},{28,16},{1,13},{... | collective-permute-start | bytes 196616 | tf_op jit(solution)/shard_map/ppermute | solution.py:180
  33.5 5.4 %collective-permute-start.11 = (bf16[32,1024]{1,0:T(8,128)(2,1)S(1)}, bf16[32,1024]{1,0:T(8,128)(2,1)S(1)}, u32[]{:S(2)}, u32[]{:S(2)}) collective-permute-start(bf16[32,1024]{1,0:T(8,128)(2,1)S(1)} %get-tuple-element.26), channel_id=1, source_target_pairs={{0,8},{4,12},{8,0},{12,4},{16,24},{20,28},{24,16},{28,20},{1,9},{5... | collective-permute-start | bytes 196616 | tf_op jit(solution)/shard_map/ppermute | solution.py:180
  33.6 5.5 %collective-permute-start.12 = (bf16[32,1024]{1,0:T(8,128)(2,1)S(1)}, bf16[32,1024]{1,0:T(8,128)(2,1)S(1)}, u32[]{:S(2)}, u32[]{:S(2)}) collective-permute-start(bf16[32,1024]{1,0:T(8,128)(2,1)S(1)} %get-tuple-element.27), channel_id=1, source_target_pairs={{0,16},{4,20},{8,24},{12,28},{16,0},{20,4},{24,8},{28,12},{1,17},{... | collective-permute-start | bytes 196616 | tf_op jit(solution)/shard_map/ppermute | solution.py:180
  37.8 4.3 %collective-permute-start.13 = (bf16[32,1024]{1,0:T(8,128)(2,1)S(1)}, bf16[32,1024]{1,0:T(8,128)(2,1)S(1)}, u32[]{:S(2)}, u32[]{:S(2)}) collective-permute-start(bf16[32,1024]{1,0:T(8,128)(2,1)S(1)} %get-tuple-element.28), channel_id=1, source_target_pairs={{0,4},{4,0},{8,12},{12,8},{16,20},{20,16},{24,28},{28,24},{1,5},{5... | collective-permute-start | bytes 196616 | tf_op jit(solution)/shard_map/ppermute | solution.py:180
  39.1 3.0 %copy-start.4 = (bf16[32,8192]{1,0:T(8,128)(2,1)}, bf16[32,8192]{1,0:T(8,128)(2,1)S(1)}, u32[]{:S(2)}) copy-start(bf16[32,8192]{1,0:T(8,128)(2,1)S(1)} %constant_dynamic-update-slice_fusion.1) | copy-start | bytes 1572868
